TPU v7x, 32 devices: a whole 2x2x4 slice. The times are simulated.
32 devices in a mesh: groups: 2 (over x), rows: 16 (over z, y, core).
Axes of the slice: x: 2, y: 2, z: 4, core: 2. Of those that a mesh axis runs over, the one named last changes fastest.
Arguments:
- images: bfloat16 [32, 64, 3, 256], P('groups', 'rows'), parts along dimension 0, may hold values from -50 to 50
- shifts: int32 [32, 12], P('groups'), parts along dimension 0, may hold values from -48 to 48, as said below
- in_weight: bfloat16 [3, 3, 32, 3], replicated, may hold values from -1.25 to 1.25
- norm_gain: float32 [32], replicated, may hold values from 0.1 to 1.9
- norm_bias: float32 [32], replicated, may hold values from -3 to 3
- mid_weight: bfloat16 [3, 3, 32, 32], replicated, may hold values from -0.375 to 0.375
- out_weight: bfloat16 [3, 3, 32, 32], replicated, may hold values from -0.375 to 0.375
- cost_weight_a: bfloat16 [3, 3, 3, 32, 32], replicated, may hold values from -0.21875 to 0.21875
- cost_weight_b: bfloat16 [3, 3, 3, 32, 32], replicated, may hold values from -0.21875 to 0.21875
Outputs:
- regularized: bfloat16 [24, 64, 32, 256], P('groups', 'rows'), parts along dimension 0
There are 2 independent parts, one for each index of `groups`. A program takes and returns all parts, laid end to end along the dimension named above; an argument that names none is the same for every part. Nothing has to cross between parts.
Inputs may be any that keep to these rules, and one draw needn't show every extreme that they name: `shifts`: the shift of camera v at plane k is b_v * (k + 1) for an integer baseline b_v of -4 to 4; some camera has b_v = 4 and another b_v = -4.
All inputs are finite; a program needn't handle non-finite values.
Results may differ from a plain program's by a relative error of at most 0.0076.
Values may be sent and summed in bfloat16 or wider, within the bound.
No kernel may reach another device: no remote copies, remote signals or barrier semaphores. Data moves between devices by JAX's collectives and lax.ppermute only.
A program may use at most 128 MiB of HBM per device.

v0:
```python
import functools
import jax
import jax.numpy as jnp
import numpy as np
from jax import lax
from jax.experimental import pallas as pl
from jax.experimental.pallas import tpu as pltpu
from jax.sharding import PartitionSpec as P

BF = jnp.bfloat16
F32 = jnp.float32
VMEM = pl.BlockSpec(memory_space=pltpu.VMEM)
SMEM = pl.BlockSpec(memory_space=pltpu.SMEM)
REACH = 48


def dot(a, b):
    return jnp.dot(a, b, preferred_element_type=F32)


def fold(sums):
    sums = sums + pltpu.roll(sums, 64, 1)
    return sums + pltpu.roll(sums, 32, 1)


def stats_kernel(x_ref, w_ref, pt_ref, st_ref, p_scr, t_scr, raw_scr):
    views, _, width = x_ref.shape
    lane = lax.broadcasted_iota(jnp.int32, (1, width), 1)
    p_scr[...] = jnp.zeros_like(p_scr)

    def one_view(v, carry):
        x = x_ref[v]
        before = jnp.where(lane == 0, 0.0, pltpu.roll(x, 1, 1))
        after = jnp.where(lane == width - 1, 0.0, pltpu.roll(x, width - 1, 1))
        p_scr[0:42, :] = before[0:42]
        p_scr[42:84, :] = x[0:42]
        p_scr[84:126, :] = after[0:42]
        t_scr[pl.ds(v, width, stride=views), :] = p_scr[...].T
        return carry

    lax.fori_loop(0, views, one_view, 0)
    chunk = 512
    steps = views * width // chunk

    def first(i, total):
        rows = pl.ds(pl.multiple_of(i * chunk, chunk), chunk)
        patch = t_scr[rows, :].astype(BF)
        pt_ref[rows, :] = patch
        raw = dot(patch, w_ref[...])
        raw_scr[rows, :] = raw
        return total + jnp.sum(raw.reshape(chunk // views, views, 128), axis=0)

    total = lax.fori_loop(0, steps, first, jnp.zeros((views, 128), F32))
    mean = fold(total) * (1.0 / (4 * width))

    def second(i, total):
        rows = pl.ds(pl.multiple_of(i * chunk, chunk), chunk)
        raw = raw_scr[rows, :].reshape(chunk // views, views, 128) - mean[None]
        return total + jnp.sum(raw * raw, axis=0)

    squares = lax.fori_loop(0, steps, second, jnp.zeros((views, 128), F32))
    st_ref[0:views, :] = mean
    st_ref[views:, :] = fold(squares)


def row_mask(info, first, lanes):
    row = info[0] + first + lax.broadcasted_iota(jnp.int32, (1, lanes), 1) // 32
    return jnp.where((row >= 0) & (row < info[1]), 1.0, 0.0).astype(F32)


def feature_kernel(info, pt_ref, st_ref, gb_ref, w1_ref, w2_ref, w3_ref, f_ref, nb, mid):
    views = st_ref.shape[0] // 2
    total = pt_ref.shape[0]
    size = 256
    cols = size // views
    steps = total // size
    mean = st_ref[0:views, :]
    count = (info[1] * (total // views)).astype(F32)
    scale = gb_ref[0:1, :] / jnp.sqrt(st_ref[views:, :] / count + 1e-05)
    shift = gb_ref[1:2, :]
    edge = jnp.zeros((views, 384), BF)
    nb[0:views, :] = edge
    nb[views + total :, :] = edge
    for block in range(2):
        mid[block, 0:views, :] = edge[:, :256]
        mid[block, views + total :, :] = edge[:, :256]

    def normalize(i, carry):
        rows = pl.ds(pl.multiple_of(i * size, size), size)
        out = pl.ds(pl.multiple_of(i * size + views, views), size)
        raw = dot(pt_ref[rows, :], w1_ref[...])
        for group in range(3):
            mask = row_mask(info, 4 * group - 4, 128)
            part = raw[:, group * 128 : group * 128 + 128].reshape(cols, views, 128)
            part = jnp.maximum((part - mean[None]) * scale[None] + shift[None], 0.0) * mask[None]
            nb[out, group * 128 : group * 128 + 128] = part.reshape(size, 128).astype(BF)
        return carry

    lax.fori_loop(0, steps, normalize, 0)

    def middle(i, carry):
        out = pl.ds(pl.multiple_of(i * size + views, views), size)
        for block in range(2):
            taps = [
                nb[pl.ds(pl.multiple_of(i * size + b * views, views), size), block * 128 : block * 128 + 256]
                for b in range(3)
            ]
            part = dot(jnp.concatenate(taps, axis=1), w2_ref[...])
            part = jnp.maximum(part, 0.0) * row_mask(info, 4 * block - 3, 256)
            mid[block, out, :] = part.astype(BF)
        return carry

    lax.fori_loop(0, steps, middle, 0)

    def last(i, carry):
        for block in range(2):
            taps = [mid[block, pl.ds(pl.multiple_of(i * size + b * views, views), size), :] for b in range(3)]
            part = dot(jnp.concatenate(taps, axis=1), w3_ref[...])
            part = (part * row_mask(info, 4 * block - 2, 128)).astype(BF).astype(F32)
            f_ref[pl.ds(pl.multiple_of(block * total + i * size, size), size), :] = part
        return carry

    lax.fori_loop(0, steps, last, 0)


def volume_kernel(info, base, f_ref, ca_ref, cb_ref, out_ref, s_scr, q_scr, v32, vb, hb):
    views = base.shape[0]
    planes = out_ref.shape[0]
    width = out_ref.shape[3]
    total = views * width
    s_scr[...] = jnp.zeros_like(s_scr)
    q_scr[...] = jnp.zeros_like(q_scr)
    for volume in (vb, hb):
        volume[0] = jnp.zeros_like(volume[0])
        volume[planes + 1] = jnp.zeros_like(volume[0])
    v32[...] = jnp.zeros_like(v32)

    def add_view(v, carry):
        step = base[v] + 4
        for block in range(2):
            feats = f_ref[pl.ds(block * total + v, width, stride=views), :]
            s_scr[block, step, REACH : REACH + width, :] += feats
            q_scr[block, step, REACH : REACH + width, :] += feats * feats
        return carry

    lax.fori_loop(0, views, add_view, 0)

    def spread_taps(dest, k):
        for tap in range(3):
            dest[k + 1, :, tap * 256 : tap * 256 + 256] = v32[7 + tap : 7 + tap + width, :].astype(BF)

    size = 32

    def one_plane(k, carry):
        for block in range(2):
            for part in range(width // size):
                start = REACH + part * size
                summed = s_scr[block, 4, start : start + size, :]
                squares = q_scr[block, 4, start : start + size, :]
                for step in (-4, -3, -2, -1, 1, 2, 3, 4):
                    rows = pl.ds(start + step * (k + 1), size)
                    summed = summed + s_scr[block, step + 4, rows, :]
                    squares = squares + q_scr[block, step + 4, rows, :]
                average = summed * (1.0 / views)
                value = squares * (1.0 / views) - average * average
                v32[8 + part * size : 8 + part * size + size, block * 128 : block * 128 + 128] = (
                    value.astype(BF).astype(F32)
                )
        spread_taps(vb, k)
        return carry

    lax.fori_loop(0, planes, one_plane, 0)
    mask = row_mask(info, -1, 256)

    def hidden(k, carry):
        value = dot(vb[k], ca_ref[0]) + dot(vb[k + 1], ca_ref[1]) + dot(vb[k + 2], ca_ref[2])
        v32[8 : 8 + width, :] = (jnp.maximum(value, 0.0) * mask).astype(BF).astype(F32)
        spread_taps(hb, k)
        return carry

    lax.fori_loop(0, planes, hidden, 0)

    def final(j, carry):
        k = 2 * j
        value = dot(hb[k], cb_ref[0]) + dot(hb[k + 1], cb_ref[1]) + dot(hb[k + 2], cb_ref[2]) + dot(hb[k + 3], cb_ref[3])
        out_ref[pl.ds(k, 2)] = value.T.astype(BF).reshape(2, 4, 32, width)
        return carry

    lax.fori_loop(0, planes // 2, final, 0)


def band(before, after, used):
    taps = np.zeros((3, before, after), np.float32)
    for row in range(used):
        for tap in range(3):
            taps[tap, row + tap, row] = 1.0
    return jnp.asarray(taps, BF)


def plane_band():
    taps = np.zeros((3, 4, 2), np.float32)
    for plane in range(2):
        for tap in range(3):
            taps[tap, plane + tap, plane] = 1.0
    return jnp.asarray(taps, BF)


def near(value, axis, step):
    count = lax.axis_size(axis)
    return lax.ppermute(value, axis, [(i, (i + step) % count) for i in range(count)])


def swap(value, axis, bit):
    count = lax.axis_size(axis)
    return lax.ppermute(value, axis, [(i, i ^ bit) for i in range(count)])


def merged_stats(stats, views, cells, axis):
    count = lax.axis_size(axis)
    bit = 1
    while bit < count:
        other = swap(stats, axis, bit)
        gap = stats[:views] - other[:views]
        mean = (stats[:views] + other[:views]) * 0.5
        squares = stats[views:] + other[views:] + gap * gap * (0.5 * cells * bit)
        stats = jnp.concatenate([mean, squares], axis=0)
        bit *= 2
    return stats


def shards(
    images,
    shifts,
    in_weight,
    norm_gain,
    norm_bias,
    mid_weight,
    out_weight,
    cost_weight_a,
    cost_weight_b,
):
    views, rows, colors, width = images.shape
    planes = shifts.shape[1]
    chan = in_weight.shape[2]
    count = lax.axis_size("rows")
    index = lax.axis_index("rows")
    core = index % 2
    total = views * width

    own = images.reshape(views, rows * colors, width)
    pair = swap(own, "rows", 1)
    upper = jnp.where(core == 0, own, pair)
    lower = jnp.where(core == 0, pair, own)
    both = jnp.concatenate([upper, lower], axis=1)
    halo = 5 * colors
    above = near(both[:, 2 * rows * colors - halo :], "rows", 2)
    below = near(both[:, :halo], "rows", -2)
    above = jnp.where(index < 2, jnp.zeros_like(above), above)
    below = jnp.where(index >= count - 2, jnp.zeros_like(below), below)
    around = jnp.concatenate([above, both, below], axis=1)
    kept = (rows + 10) * colors
    slab = jnp.where(core == 0, around[:, :kept], around[:, rows * colors :])
    slab = jnp.pad(slab, ((0, 0), (0, 48 - kept), (0, 0))).astype(F32)

    w1 = jnp.einsum("aboc,aqr->bqcro", in_weight, band(14, 12, 12)).reshape(3 * 14 * colors, 12 * chan)
    w1 = jnp.pad(w1, ((0, 2), (0, 0)))
    w2 = jnp.einsum("aboc,aqr->bqcro", mid_weight, band(8, 8, 6)).reshape(3 * 8 * chan, 8 * chan)
    w3 = jnp.einsum("aboc,aqr->bqcro", out_weight, band(8, 4, 4)).reshape(3 * 8 * chan, 4 * chan)
    ca = jnp.einsum("daboc,aqr->dbqcro", cost_weight_a, band(8, 8, 6)).reshape(3, 3 * 8 * chan, 8 * chan)
    cb = jnp.einsum("daboc,aqr->dbqcro", cost_weight_b, band(8, 4, 4))
    cb = jnp.einsum("dbqcro,dps->pbqcsro", cb, plane_band()).reshape(4, 3 * 8 * chan, 2 * 4 * chan)
    params = pltpu.CompilerParams(vmem_limit_bytes=60 * 1024 * 1024)

    patches, stats = pl.pallas_call(
        stats_kernel,
        name="stats",
        out_shape=(
            jax.ShapeDtypeStruct((total, 128), BF),
            jax.ShapeDtypeStruct((2 * views, 128), F32),
        ),
        in_specs=[VMEM] * 2,
        out_specs=(VMEM, VMEM),
        scratch_shapes=[pltpu.VMEM((128, width), F32), pltpu.VMEM((total, 128), F32), pltpu.VMEM((total, 128), F32)],
        compiler_params=params,
    )(slab, w1[:, 128:256])
    stats = merged_stats(stats, views, rows * width, "rows")

    info = jnp.stack([index * rows, count * rows]).astype(jnp.int32)
    gain_bias = jnp.tile(jnp.stack([norm_gain, norm_bias]), (1, 4))
    features = pl.pallas_call(
        feature_kernel,
        name="features",
        out_shape=jax.ShapeDtypeStruct((2 * total, 128), F32),
        in_specs=[SMEM] + [VMEM] * 6,
        out_specs=VMEM,
        scratch_shapes=[pltpu.VMEM((total + 2 * views, 384), BF), pltpu.VMEM((2, total + 2 * views, 256), BF)],
        compiler_params=params,
    )(info, patches, stats, gain_bias, w1, w2, w3)

    base = shifts[:, 0]
    return pl.pallas_call(
        volume_kernel,
        name="volume",
        out_shape=jax.ShapeDtypeStruct((planes, rows, chan, width), BF),
        in_specs=[SMEM, SMEM] + [VMEM] * 3,
        out_specs=VMEM,
        scratch_shapes=[
            pltpu.VMEM((2, 9, width + 2 * REACH, 128), F32),
            pltpu.VMEM((2, 9, width + 2 * REACH, 128), F32),
            pltpu.VMEM((width + 16, 256), F32),
            pltpu.VMEM((planes + 2, width, 768), BF),
            pltpu.VMEM((planes + 2, width, 768), BF),
        ],
        compiler_params=params,
    )(info, base, features, ca, cb)


def solution(mesh):
    placed = (P("groups", "rows", None, None), P("groups", None), P(), P(), P(), P(), P(), P(), P())
    return jax.shard_map(
        shards,
        mesh=mesh,
        in_specs=placed,
        out_specs=P("groups", "rows", None, None),
        check_vma=False,
    )
```

profile of v0, /device:TPU:0, one launch (start us, length us, event | category | flops | bytes accessed | tf_op | source)
XLA Modules:
  0.0 134.1 jit_solution(1814037282030588326)
XLA Ops:
  0.0 0.9 copy.26
  1.0 0.7 copy.28
  2.1 2.8 %fusion.2 = bf16[8,4,3,3,32,32]{5,0,4,3,2,1:T(8,128)(2,1)} fusion(bf16[3,8,4,1,1,1]{1,0,5,4,3,2:T(4,128)(2,1)} %constant.58, bf16[3,3,3,32,32,1]{4,3,2,1,0,5:T(8,128)(2,1)S(1)} %bitcast.62), kind=kOutput, calls=%fused_computation.10 | convolution fusion | flops 1769472 | bytes 645312 | tf_op jit(solution)/shard_map/daboc,aqr->dbqcro/dot_general | solution.py:270
  4.9 5.1 %copy.45 = bf16[8,4,3,3,32,32]{4,2,1,5,0,3:T(4,128)(2,1)S(1)} copy(bf16[8,4,3,3,32,32]{5,0,4,3,2,1:T(8,128)(2,1)} %fusion.2) | data formatting | bytes 1179648 | tf_op jit(solution)/shard_map/daboc,aqr->dbqcro/dot_general | solution.py:270
  10.0 5.2 %convolution_bitcast_fusion = bf16[4,3,8,32,2,4,32]{6,0,4,5,3,2,1:T(4,128)(2,1)} fusion(bf16[3,4,2,1,1,1,1]{0,1,2,6,5,4,3:T(4,128)(2,1)S(1)} %copy-done.10, bf16[8,4,3,3,32,32]{4,2,1,5,0,3:T(4,128)(2,1)S(1)} %copy.45), kind=kOutput, calls=%fused_computation | convolution fusion | flops 4718592 | bytes 2162736 | tf_op jit(solution)/shard_map/dbqcro,dps->pbqcsro/dot_general | solution.py:271
  15.3 3.5 %convolution_bitcast_fusion.1 = bf16[3,3,8,32,8,32]{3,4,5,1,0,2:T(8,128)(2,1)} fusion(bf16[3,8,8,1,1,1]{2,0,5,4,3,1:T(4,128)(2,1)S(1)} %copy-done.4, bf16[3,3,3,32,32]{4,3,2,1,0:T(8,128)(2,1)S(1)} %copy-done.1), kind=kOutput, calls=%fused_computation.2 | convolution fusion | flops 3538944 | bytes 1235328 | tf_op jit(solution)/shard_map/daboc,aqr->dbqcro/dot_general | solution.py:269
  19.5 0.9 broadcast_select_fusion.2
  20.5 2.6 %collective-permute-start.1 = (bf16[16,15,256]{2,1,0:T(8,128)(2,1)S(1)}, bf16[16,15,256]{2,1,0:T(8,128)(2,1)S(1)}, u32[]{:S(2)}, u32[]{:S(2)}) collective-permute-start(bf16[16,15,256]{2,1,0:T(8,128)(2,1)S(1)} %get-tuple-element.9), channel_id=1, source_target_pairs={{0,2},{1,3},{2,4},{3,5},{4,6},{5,7},{6,8},{7,9},{8,10},{9,11},{10,... | collective-permute-start | bytes 368648 | tf_op jit(solution)/shard_map/ppermute | solution.py:210
  24.6 3.1 %collective-permute-start.2 = (bf16[16,15,256]{2,1,0:T(8,128)(2,1)S(1)}, bf16[16,15,256]{2,1,0:T(8,128)(2,1)S(1)}, u32[]{:S(2)}, u32[]{:S(2)}) collective-permute-start(bf16[16,15,256]{2,1,0:T(8,128)(2,1)S(1)} %get-tuple-element.10), channel_id=1, source_target_pairs={{0,14},{1,15},{2,0},{3,1},{4,2},{5,3},{6,4},{7,5},{8,6},{9,7},{10,... | collective-permute-start | bytes 368648 | tf_op jit(solution)/shard_map/ppermute | solution.py:210
  27.7 2.7 %collective-permute-done.1 = bf16[16,15,256]{2,1,0:T(8,128)(2,1)S(1)} collective-permute-done((bf16[16,15,256]{2,1,0:T(8,128)(2,1)S(1)}, bf16[16,15,256]{2,1,0:T(8,128)(2,1)S(1)}, u32[]{:S(2)}, u32[]{:S(2)}) %collective-permute-start.1) | collective-permute-done | bytes 122912 | tf_op jit(solution)/shard_map/ppermute | solution.py:210
  30.4 2.6 %collective-permute-done.2 = bf16[16,15,256]{2,1,0:T(8,128)(2,1)S(1)} collective-permute-done((bf16[16,15,256]{2,1,0:T(8,128)(2,1)S(1)}, bf16[16,15,256]{2,1,0:T(8,128)(2,1)S(1)}, u32[]{:S(2)}, u32[]{:S(2)}) %collective-permute-start.2) | collective-permute-done | bytes 122912 | tf_op jit(solution)/shard_map/ppermute | solution.py:210
  33.3 1.0 pad_convert_fusion.x_ref
  34.3 7.5 %stats.1 = (bf16[4096,128]{1,0:T(8,128)(2,1)}, f32[32,128]{1,0:T(8,128)}) custom-call(f32[16,48,256]{2,1,0:T(8,128)} %pad_convert_fusion.x_ref, bf16[128,128]{1,0:T(8,128)(2,1)} %pad_slice_fusion.2.w_ref), custom_call_target="tpu_custom_call" | custom-call | tf_op jit(solution)/shard_map/stats/pallas_call | solution.py:274
  41.8 1.3 convolution_bitcast_fusion.3
  43.2 0.7 add_multiply_fusion.3
  44.0 0.7 slice_reduce_fusion.base
  44.7 3.0 %collective-permute-done.4 = f32[32,128]{1,0:T(8,128)S(1)} collective-permute-done((f32[32,128]{1,0:T(8,128)S(1)}, f32[32,128]{1,0:T(8,128)S(1)}, u32[]{:S(2)}, u32[]{:S(2)}) %collective-permute-start.4) | collective-permute-done | bytes 16416 | tf_op jit(solution)/shard_map/ppermute | solution.py:215
  47.8 3.7 %collective-permute-done.5 = f32[32,128]{1,0:T(8,128)S(1)} collective-permute-done((f32[32,128]{1,0:T(8,128)S(1)}, f32[32,128]{1,0:T(8,128)S(1)}, u32[]{:S(2)}, u32[]{:S(2)}) %collective-permute-start.5) | collective-permute-done | bytes 16416 | tf_op jit(solution)/shard_map/ppermute | solution.py:215
  51.5 0.8 collective-permute-start.6
  52.3 0.6 pad_add_fusion.info
  53.0 0.6 pad.9.w1_ref
  53.6 1.4 %copy.33 = bf16[3,8,32,8,32]{4,3,2,1,0:T(8,128)(2,1)S(1)} copy(bf16[3,8,32,8,32]{2,3,4,0,1:T(8,128)(2,1)S(1)} %convolution_bitcast_fusion.2) | data formatting | bytes 786432 | tf_op jit(solution)/shard_map/aboc,aqr->bqcro/transpose | solution.py:267
  55.0 1.9 %reshape.24.w2_ref = bf16[768,256]{1,0:T(8,128)(2,1)} reshape(bf16[3,8,32,8,32]{4,3,2,1,0:T(8,128)(2,1)S(1)} %copy.33) | data formatting | bytes 786432 | tf_op jit(solution)/shard_map/reshape | solution.py:267
  56.9 2.2 %copy.35 = bf16[3,8,32,4,32]{4,3,2,1,0:T(4,128)(2,1)S(1)} copy(bf16[3,8,32,4,32]{2,1,4,0,3:T(8,128)(2,1)} %convolution_bitcast_fusion.3) | data formatting | bytes 393216 | tf_op jit(solution)/shard_map/aboc,aqr->bqcro/transpose | solution.py:268
  59.1 1.1 reshape.25.w3_ref
  60.2 0.6 tile.10.gb_ref
  60.8 9.0 %copy.38 = bf16[4,3,8,32,2,4,32]{6,5,4,3,2,1,0:T(4,128)(2,1)} copy(bf16[4,3,8,32,2,4,32]{6,0,4,5,3,2,1:T(4,128)(2,1)} %convolution_bitcast_fusion) | data formatting | bytes 3145728 | tf_op jit(solution)/shard_map/dbqcro,dps->pbqcsro/transpose | solution.py:271
  69.9 9.7 %reshape.27.cb_ref = bf16[4,768,256]{2,1,0:T(8,128)(2,1)} reshape(bf16[4,3,8,32,2,4,32]{6,5,4,3,2,1,0:T(4,128)(2,1)} %copy.38) | data formatting | bytes 3145728 | tf_op jit(solution)/shard_map/reshape | solution.py:271
  79.5 7.4 %copy.37 = bf16[3,3,8,32,8,32]{5,4,3,2,1,0:T(8,128)(2,1)} copy(bf16[3,3,8,32,8,32]{3,4,5,1,0,2:T(8,128)(2,1)} %convolution_bitcast_fusion.1) | data formatting | bytes 2359296 | tf_op jit(solution)/shard_map/daboc,aqr->dbqcro/transpose | solution.py:269
  86.9 6.6 %reshape.26.ca_ref = bf16[3,768,256]{2,1,0:T(8,128)(2,1)} reshape(bf16[3,3,8,32,8,32]{5,4,3,2,1,0:T(8,128)(2,1)} %copy.37) | data formatting | bytes 2359296 | tf_op jit(solution)/shard_map/reshape | solution.py:269
  94.1 18.8 %features.1.f_ref = f32[8192,128]{1,0:T(8,128)} custom-call(s32[2]{0:T(128)} %pad_add_fusion.info, bf16[4096,128]{1,0:T(8,128)(2,1)} %get-tuple-element.7.pt_ref, f32[32,128]{1,0:T(8,128)} %pad_maximum_fusion.5.st_ref, f32[2,128]{1,0:T(2,128)} %tile.10.gb_ref, bf16[128,384]{1,0:T(8,128)(2,1)} %pad.9.w1_ref, bf16[768,256]{1,0:T(8,128)(2,1)} %reshape.24.w2_ref, ...), custom_call_target="tpu_custom_call" | custom-call | tf_op jit(solution)/shard_map/features/pallas_call | solution.py:290
  113.0 21.1 %volume.1 = bf16[12,4,32,256]{3,2,1,0:T(8,128)(2,1)} custom-call(s32[2]{0:T(128)} %pad_add_fusion.info, s32[16]{0:T(128)} %slice_reduce_fusion.base, f32[8192,128]{1,0:T(8,128)} %features.1.f_ref, bf16[3,768,256]{2,1,0:T(8,128)(2,1)} %reshape.26.ca_ref, bf16[4,768,256]{2,1,0:T(8,128)(2,1)} %reshape.27.cb_ref), custom_call_target="tpu_custom_call" | custom-call | tf_op jit(solution)/shard_map/volume/pallas_call | solution.py:301
  (52 shorter events, 3.8 us)
Async XLA Ops:
  0.0 2.1 %copy-start = (bf16[3,3,3,32,32]{4,3,2,1,0:T(8,128)(2,1)S(1)}, bf16[3,3,3,32,32]{4,3,2,1,0:T(8,128)(2,1)}, u32[]{:S(2)}) copy-start(bf16[3,3,3,32,32]{4,3,2,1,0:T(8,128)(2,1)} %param.23) | copy-start | bytes 165892
  1.6 17.8 %collective-permute-start = (bf16[16,12,256]{2,1,0:T(8,128)(2,1)}, bf16[16,12,256]{2,1,0:T(8,128)(2,1)}, u32[]{:S(2)}, u32[]{:S(2)}) collective-permute-start(bf16[16,12,256]{2,1,0:T(8,128)(2,1)} %copy.28), channel_id=1, source_target_pairs={{0,1},{1,0},{2,3},{3,2},{4,5},{5,4},{6,7},{7,6},{8,9},{9,8},{10,11... | collective-permute-start | bytes 294920 | tf_op jit(solution)/shard_map/ppermute | solution.py:215
  4.9 5.1 %copy-start.10 = (bf16[3,4,2,1,1,1,1]{0,1,2,6,5,4,3:T(4,128)(2,1)S(1)}, bf16[3,4,2,1,1,1,1]{0,1,2,6,5,4,3:T(4,128)(2,1)}, u32[]{:S(2)}) copy-start(bf16[3,4,2,1,1,1,1]{0,1,2,6,5,4,3:T(4,128)(2,1)} %constant.59) | copy-start | bytes 148
  10.0 5.2 %copy-start.1 = (bf16[3,3,3,32,32]{4,3,2,1,0:T(8,128)(2,1)S(1)}, bf16[3,3,3,32,32]{4,3,2,1,0:T(8,128)(2,1)}, u32[]{:S(2)}) copy-start(bf16[3,3,3,32,32]{4,3,2,1,0:T(8,128)(2,1)} %param.22) | copy-start | bytes 165892
  10.0 5.2 %copy-start.4 = (bf16[3,8,8,1,1,1]{2,0,5,4,3,1:T(4,128)(2,1)S(1)}, bf16[3,8,8,1,1,1]{2,0,5,4,3,1:T(4,128)(2,1)}, u32[]{:S(2)}) copy-start(bf16[3,8,8,1,1,1]{2,0,5,4,3,1:T(4,128)(2,1)} %constant.57) | copy-start | bytes 1156
  15.2 3.6 %copy-start.2 = (bf16[3,3,32,32]{3,2,1,0:T(8,128)(2,1)S(1)}, bf16[3,3,32,32]{3,2,1,0:T(8,128)(2,1)}, u32[]{:S(2)}) copy-start(bf16[3,3,32,32]{3,2,1,0:T(8,128)(2,1)} %param.20) | copy-start | bytes 55300
  15.2 3.6 %copy-start.7 = (bf16[3,8,8,1,1]{2,0,4,3,1:T(4,128)(2,1)S(1)}, bf16[3,8,8,1,1]{2,0,4,3,1:T(4,128)(2,1)}, u32[]{:S(2)}) copy-start(bf16[3,8,8,1,1]{2,0,4,3,1:T(4,128)(2,1)} %constant.55) | copy-start | bytes 1156
  15.2 7.8 %copy-start.5 = (bf16[3,14,12,1,1]{1,0,4,3,2:T(4,128)(2,1)S(1)}, bf16[3,14,12,1,1]{1,0,4,3,2:T(4,128)(2,1)}, u32[]{:S(2)}) copy-start(bf16[3,14,12,1,1]{1,0,4,3,2:T(4,128)(2,1)} %constant.54) | copy-start | bytes 3028
  15.3 7.8 %copy-start.6 = (bf16[3,3,32,3]{2,3,1,0:T(4,128)(2,1)S(1)}, bf16[3,3,32,3]{2,3,1,0:T(4,128)(2,1)}, u32[]{:S(2)}) copy-start(bf16[3,3,32,3]{2,3,1,0:T(4,128)(2,1)} %param.17) | copy-start | bytes 5188
  20.5 9.9 %collective-permute-start.1 = (bf16[16,15,256]{2,1,0:T(8,128)(2,1)S(1)}, bf16[16,15,256]{2,1,0:T(8,128)(2,1)S(1)}, u32[]{:S(2)}, u32[]{:S(2)}) collective-permute-start(bf16[16,15,256]{2,1,0:T(8,128)(2,1)S(1)} %get-tuple-element.9), channel_id=1, source_target_pairs={{0,2},{1,3},{2,4},{3,5},{4,6},{5,7},{6,8},{7,9},{8,10},{9,11},{10,... | collective-permute-start | bytes 368648 | tf_op jit(solution)/shard_map/ppermute | solution.py:210
  23.4 18.4 %copy-start.3 = (bf16[3,3,32,32]{3,2,1,0:T(8,128)(2,1)S(1)}, bf16[3,3,32,32]{3,2,1,0:T(8,128)(2,1)}, u32[]{:S(2)}) copy-start(bf16[3,3,32,32]{3,2,1,0:T(8,128)(2,1)} %param.21) | copy-start | bytes 55300
  23.4 18.3 %copy-start.9 = (bf16[3,8,4,1,1]{1,0,4,3,2:T(4,128)(2,1)S(1)}, bf16[3,8,4,1,1]{1,0,4,3,2:T(4,128)(2,1)}, u32[]{:S(2)}) copy-start(bf16[3,8,4,1,1]{1,0,4,3,2:T(4,128)(2,1)} %constant.56) | copy-start | bytes 580
  23.6 20.4 %copy-start.8 = (s32[16,12]{1,0:T(8,128)S(1)}, s32[16,12]{1,0:T(8,128)}, u32[]{:S(2)}) copy-start(s32[16,12]{1,0:T(8,128)} %param.16) | copy-start | bytes 2308
  23.6 24.2 %copy-start.11 = (f32[32]{0:T(128)S(1)}, f32[32]{0:T(128)}, u32[]{:S(2)}) copy-start(f32[32]{0:T(128)} %param.19) | copy-start | bytes 388
  23.6 24.2 %copy-start.12 = (f32[32]{0:T(128)S(1)}, f32[32]{0:T(128)}, u32[]{:S(2)}) copy-start(f32[32]{0:T(128)} %param.18) | copy-start | bytes 388
  24.6 8.4 %collective-permute-start.2 = (bf16[16,15,256]{2,1,0:T(8,128)(2,1)S(1)}, bf16[16,15,256]{2,1,0:T(8,128)(2,1)S(1)}, u32[]{:S(2)}, u32[]{:S(2)}) collective-permute-start(bf16[16,15,256]{2,1,0:T(8,128)(2,1)S(1)} %get-tuple-element.10), channel_id=1, source_target_pairs={{0,14},{1,15},{2,0},{3,1},{4,2},{5,3},{6,4},{7,5},{8,6},{9,7},{10,... | collective-permute-start | bytes 368648 | tf_op jit(solution)/shard_map/ppermute | solution.py:210
  41.8 1.4 %collective-permute-start.3 = (f32[32,128]{1,0:T(8,128)}, f32[32,128]{1,0:T(8,128)S(1)}, u32[]{:S(2)}, u32[]{:S(2)}) collective-permute-start(f32[32,128]{1,0:T(8,128)} %get-tuple-element.8), channel_id=1, source_target_pairs={{0,1},{1,0},{2,3},{3,2},{4,5},{5,4},{6,7},{7,6},{8,9},{9,8},{10,11... | collective-permute-start | bytes 49160 | tf_op jit(solution)/shard_map/ppermute | solution.py:215
  43.9 3.8 %collective-permute-start.4 = (f32[32,128]{1,0:T(8,128)S(1)}, f32[32,128]{1,0:T(8,128)S(1)}, u32[]{:S(2)}, u32[]{:S(2)}) collective-permute-start(f32[32,128]{1,0:T(8,128)S(1)} %pad_maximum_fusion.2), channel_id=1, source_target_pairs={{0,2},{1,3},{2,0},{3,1},{4,6},{5,7},{6,4},{7,5},{8,10},{9,11},{10,... | collective-permute-start | bytes 49160 | tf_op jit(solution)/shard_map/ppermute | solution.py:215
  47.7 3.8 %collective-permute-start.5 = (f32[32,128]{1,0:T(8,128)S(1)}, f32[32,128]{1,0:T(8,128)S(1)}, u32[]{:S(2)}, u32[]{:S(2)}) collective-permute-start(f32[32,128]{1,0:T(8,128)S(1)} %pad_maximum_fusion.3), channel_id=1, source_target_pairs={{0,4},{1,5},{2,6},{3,7},{4,0},{5,1},{6,2},{7,3},{8,12},{9,13},{10,... | collective-permute-start | bytes 49160 | tf_op jit(solution)/shard_map/ppermute | solution.py:215
  51.5 42.0 %collective-permute-start.6 = (f32[32,128]{1,0:T(8,128)S(1)}, f32[32,128]{1,0:T(8,128)S(1)}, u32[]{:S(2)}, u32[]{:S(2)}) collective-permute-start(f32[32,128]{1,0:T(8,128)S(1)} %pad_maximum_fusion.4), channel_id=1, source_target_pairs={{0,8},{1,9},{2,10},{3,11},{4,12},{5,13},{6,14},{7,15},{8,0},{9,1},... | collective-permute-start | bytes 49160 | tf_op jit(solution)/shard_map/ppermute | solution.py:215
where the time goes:
time: 135 us; the launch traced here: 134 us
  local copies, waits for them, and re-layouts  49.1 us (36%)
  Pallas kernels  47.4 us (35%)
  matrix products  13.8 us (10%)
  waiting for transfers between devices  12.1 us (9%)
  starting transfers between devices  7.02 us (5%)
  other arithmetic  4.32 us (3%)
    pallas_call x1, Pallas kernels, shards(): pl.pallas_call(volume_kernel, name='volume', out_shape=jax.ShapeDtypeStru...  21.1 us
    pallas_call x1, Pallas kernels, shards(): pl.pallas_call(feature_kernel, name='features', out_shape=jax.ShapeDtypeS...  18.8 us
    reshape x1, local copies, waits for them, and re-layouts, shards(): jnp.einsum('dbqcro,dps->pbqcsro', cb, plane_band())  9.66 us
    transpose x1, local copies, waits for them, and re-layouts, shards(): jnp.einsum('dbqcro,dps->pbqcsro', cb, plane_band())  9.02 us
    pallas_call x1, Pallas kernels, shards(): pl.pallas_call(stats_kernel, name='stats', out_shape=(jax.ShapeDtypeStruc...  7.47 us
    transpose x1, local copies, waits for them, and re-layouts, shards(): jnp.einsum('daboc,aqr->dbqcro', cost_weight_a, band(8, 8, 6))  7.41 us
    ppermute x5, waiting for transfers between devices, swap(): return lax.ppermute(value, axis, [(i, i ^ bit) for i in range(count)])  6.79 us
    reshape x1, local copies, waits for them, and re-layouts, shards(): jnp.einsum('daboc,aqr->dbqcro', cost_weight_a, band(8, 8, 6))  6.58 us
  transfers between devices with their start and end apart: 7, of which 5 were waited for; matrix products, arithmetic and copies ran while one was open for 46% of the time, Pallas kernels for 0%

commit v1 on v0

v1 whole, which is shorter than its diff:
```python
import functools
import jax
import jax.numpy as jnp
from jax import lax
from jax.experimental import pallas as pl
from jax.experimental.pallas import tpu as pltpu
from jax.sharding import PartitionSpec as P

BF = jnp.bfloat16
F32 = jnp.float32
VMEM = pl.BlockSpec(memory_space=pltpu.VMEM)
SMEM = pl.BlockSpec(memory_space=pltpu.SMEM)
REACH = 48


def dot(a, b):
    return jnp.dot(a, b, preferred_element_type=F32)


def fold(sums):
    sums = sums + pltpu.roll(sums, 64, 1)
    return sums + pltpu.roll(sums, 32, 1)


def stats_kernel(both_ref, above_ref, below_ref, w_ref, pt_ref, st_ref, x_scr, p_scr, t_scr, raw_scr):
    views, tall, width = both_ref.shape
    halo = above_ref.shape[1]
    index = lax.axis_index("rows")
    core = index % 2
    top = (index >= 2).astype(F32)
    bottom = (index < lax.axis_size("rows") - 2).astype(F32)
    lane = lax.broadcasted_iota(jnp.int32, (1, width), 1)
    p_scr[...] = jnp.zeros_like(p_scr)
    x_scr[...] = jnp.zeros_like(x_scr)
    slots = p_scr.shape[0]

    def some_views(i, carry):
        for slot in range(slots):
            v = i * slots + slot
            x_scr[slot, 0:halo, :] = above_ref[v].astype(F32) * top
            x_scr[slot, halo : halo + tall, :] = both_ref[v].astype(F32)
            x_scr[slot, halo + tall : 2 * halo + tall, :] = below_ref[v].astype(F32) * bottom
            x = jnp.where(core == 0, x_scr[slot, 0:48, :], x_scr[slot, 12:60, :])
            before = jnp.where(lane == 0, 0.0, pltpu.roll(x, 1, 1))
            after = jnp.where(lane == width - 1, 0.0, pltpu.roll(x, width - 1, 1))
            p_scr[slot, 0:42, :] = before[0:42]
            p_scr[slot, 42:84, :] = x[0:42]
            p_scr[slot, 84:126, :] = after[0:42]
            t_scr[pl.ds(v, width, stride=views), :] = p_scr[slot].T
        return carry

    lax.fori_loop(0, views // slots, some_views, 0)
    chunk = 1024
    steps = views * width // chunk
    weight = w_ref[:, pl.ds(pl.multiple_of(128 - 128 * core, 128), 256)]

    def first(i, total):
        rows = pl.ds(pl.multiple_of(i * chunk, chunk), chunk)
        patch = t_scr[rows, :].astype(BF)
        pt_ref[rows, :] = patch
        raw = dot(patch, weight)
        raw_scr[rows, :] = raw
        return total + jnp.sum(raw.reshape(chunk // views, views, 256), axis=0)

    total = lax.fori_loop(0, steps, first, jnp.zeros((views, 256), F32))
    mean = fold(total[:, :128] + total[:, 128:]) * (1.0 / (8 * width))

    def second(i, total):
        rows = pl.ds(pl.multiple_of(i * chunk, chunk), chunk)
        raw = raw_scr[rows, :].reshape(chunk // views, views, 256)
        for half in range(2):
            part = raw[:, :, half * 128 : half * 128 + 128] - mean[None]
            total = total + jnp.sum(part * part, axis=0)
        return total

    squares = lax.fori_loop(0, steps, second, jnp.zeros((views, 128), F32))
    st_ref[0:views, :] = mean
    st_ref[views:, :] = fold(squares)


def row_mask(first, lanes):
    row = lax.axis_index("rows") * 4 + first + lax.broadcasted_iota(jnp.int32, (1, lanes), 1) // 32
    return jnp.where((row >= 0) & (row < lax.axis_size("rows") * 4), 1.0, 0.0).astype(F32)


def merge(one, two, views, cells):
    gap = one[:views] - two[:views]
    mean = (one[:views] + two[:views]) * 0.5
    return mean, one[views:] + two[views:] + gap * gap * (0.5 * cells)


def tiled_lanes(scr, ref):
    scr[...] = jnp.zeros_like(scr)
    scr[0:1, 0:32] = ref[...]
    return fold(scr[...])[0:1]


def main_kernel(
    shifts, pt_ref, st_ref, other_ref, gain_ref, bias_ref, w1_ref, w2_ref, w3_ref, ca_hbm, cb_hbm, out_ref,
    nb, mid, f_scr, s_scr, q_scr, v32, vb, hb, ca_ref, cb_ref, g_scr, sems,
):
    copies = [
        pltpu.make_async_copy(ca_hbm, ca_ref, sems.at[0]),
        pltpu.make_async_copy(cb_hbm, cb_ref, sems.at[1]),
    ]
    for copy in copies:
        copy.start()
    views = st_ref.shape[0] // 2
    total = pt_ref.shape[0]
    planes = out_ref.shape[0]
    width = out_ref.shape[3]
    cells = lax.axis_size("rows") * 4 * width
    mean, squares = merge(st_ref[...], other_ref[...], views, cells // 2)
    scale = tiled_lanes(g_scr, gain_ref) / jnp.sqrt(squares * (1.0 / cells) + 1e-05)
    shift = tiled_lanes(g_scr, bias_ref)
    edge = jnp.zeros((views, 384), BF)
    nb[0:views, :] = edge
    nb[views + total :, :] = edge
    for block in range(2):
        mid[block, 0:views, :] = edge[:, :256]
        mid[block, views + total :, :] = edge[:, :256]
    size = 1024
    cols = size // views
    steps = total // size
    masks = [row_mask(4 * group - 4, 128) for group in range(3)]

    def normalize(i, carry):
        rows = pl.ds(pl.multiple_of(i * size, size), size)
        out = pl.ds(pl.multiple_of(i * size + views, views), size)
        raw = dot(pt_ref[rows, :], w1_ref[...])
        for group in range(3):
            part = raw[:, group * 128 : group * 128 + 128].reshape(cols, views, 128)
            part = jnp.maximum((part - mean[None]) * scale[None] + shift[None], 0.0) * masks[group][None]
            nb[out, group * 128 : group * 128 + 128] = part.reshape(size, 128).astype(BF)
        return carry

    lax.fori_loop(0, steps, normalize, 0)
    mid_masks = [row_mask(4 * block - 3, 256) for block in range(2)]

    def middle(i, carry):
        out = pl.ds(pl.multiple_of(i * size + views, views), size)
        for block in range(2):
            taps = [
                nb[pl.ds(pl.multiple_of(i * size + b * views, views), size), block * 128 : block * 128 + 256]
                for b in range(3)
            ]
            part = dot(jnp.concatenate(taps, axis=1), w2_ref[...])
            part = jnp.maximum(part, 0.0) * mid_masks[block]
            mid[block, out, :] = part.astype(BF)
        return carry

    lax.fori_loop(0, steps, middle, 0)
    last_masks = [row_mask(4 * block - 2, 128) for block in range(2)]
    couples = 32

    def last(i, carry):
        for block in range(2):
            rows = pl.ds(pl.multiple_of(i * couples * 2 * views, 2 * views), (couples + 1) * 2 * views)
            value = mid[block, rows, :].reshape(couples + 1, 2, views, 256)
            taps = [value[j // 2 : j // 2 + couples, j % 2].reshape(couples * views, 256) for j in range(4)]
            part = dot(jnp.concatenate(taps, axis=1), w3_ref[...])
            halves = [
                (part[:, q * 128 : q * 128 + 128] * last_masks[block]).astype(BF).astype(F32).reshape(couples, 1, views, 128)
                for q in range(2)
            ]
            start = pl.multiple_of(block * total + i * couples * 2 * views, 2 * views)
            f_scr[pl.ds(start, couples * 2 * views), :] = jnp.concatenate(halves, axis=1).reshape(couples * 2 * views, 128)
        return carry

    lax.fori_loop(0, width // 2 // couples, last, 0)

    s_scr[...] = jnp.zeros_like(s_scr)
    q_scr[...] = jnp.zeros_like(q_scr)
    for pair in (0, planes // 2):
        hb[pair, pair * 2 // planes] = jnp.zeros_like(hb[0, 0])
    vb[0] = jnp.zeros_like(vb[0])
    vb[planes + 1] = jnp.zeros_like(vb[0])
    v32[...] = jnp.zeros_like(v32)

    def add_view(v, carry):
        step = shifts[v, 0] + 4
        for block in range(2):
            feats = f_scr[pl.ds(block * total + v, width, stride=views), :]
            s_scr[block, step, REACH : REACH + width, :] += feats
            q_scr[block, step, REACH : REACH + width, :] += feats * feats
        return carry

    lax.fori_loop(0, views, add_view, 0)
    part_size = 32

    def one_plane(k, carry):
        for block in range(2):
            for part in range(width // part_size):
                start = REACH + part * part_size
                summed = s_scr[block, 4, start : start + part_size, :]
                squares = q_scr[block, 4, start : start + part_size, :]
                for step in (-4, -3, -2, -1, 1, 2, 3, 4):
                    rows = pl.ds(start + step * (k + 1), part_size)
                    summed = summed + s_scr[block, step + 4, rows, :]
                    squares = squares + q_scr[block, step + 4, rows, :]
                average = summed * (1.0 / views)
                value = (squares * (1.0 / views) - average * average).astype(BF)
                v32[0, 8 + part * part_size : 8 + part * part_size + part_size, block * 128 : block * 128 + 128] = (
                    value.astype(F32)
                )
        for tap in range(3):
            vb[k + 1, :, tap * 256 : tap * 256 + 256] = v32[0, 7 + tap : 7 + tap + width, :].astype(BF)
        return carry

    lax.fori_loop(0, planes, one_plane, 0)
    mask = row_mask(-1, 256)
    group = v32.shape[0]
    copies[0].wait()

    def hidden(i, carry):
        k = i * group
        value = sum(dot(vb[pl.ds(k + d, group)].reshape(group * width, 768), ca_ref[d]) for d in range(3))
        value = (jnp.maximum(value, 0.0) * mask).astype(BF).astype(F32)
        for t in range(group):
            v32[t, 8 : 8 + width, :] = value[t * width : (t + 1) * width]
            plane = k + t + 1
            for tap in range(3):
                hb[plane // 2, plane % 2, :, tap * 256 : tap * 256 + 256] = v32[t, 7 + tap : 7 + tap + width, :].astype(BF)
        return carry

    lax.fori_loop(0, planes // group, hidden, 0)
    pairs = 3
    copies[1].wait()

    def final(i, carry):
        j = i * pairs
        value = sum(
            dot(hb[pl.ds(j + p // 2, pairs), p % 2].reshape(pairs * width, 768), cb_ref[p]) for p in range(4)
        )
        for t in range(pairs):
            part = value[t * width : (t + 1) * width].T
            out_ref[pl.ds(2 * (j + t), 2)] = part.astype(BF).reshape(2, 4, 32, width)
        return carry

    lax.fori_loop(0, planes // 2 // pairs, final, 0)


def one_hot(rows, lanes, same):
    row = lax.broadcasted_iota(jnp.int32, (rows, lanes), 0)
    lane = lax.broadcasted_iota(jnp.int32, (rows, lanes), 1)
    return jnp.where(same(row, lane), 1.0, 0.0)


def tiled_blocks(w_ref, index, eye):
    return [
        lax.dot_general(w_ref[index(a)], eye, (((0,), (0,)), ((), ())), preferred_element_type=F32) for a in range(3)
    ]


def banded(blocks, row_in, used):
    group = lax.broadcasted_iota(jnp.int32, blocks[0].shape, 1) // 32
    value = jnp.zeros_like(blocks[0])
    for a in range(3):
        if 0 <= row_in - a < used:
            value = jnp.where(group == row_in - a, blocks[a], value)
    return value.astype(BF)


def small_weights_kernel(win_ref, wmid_ref, wout_ref, w1_ref, w2_ref, w3_ref):
    eye = one_hot(32, 384, lambda row, lane: row == lane % 32).astype(BF)
    colors = dot(win_ref[...], eye).astype(BF)
    value = jnp.zeros((128, 384), F32)
    row = lax.broadcasted_iota(jnp.int32, (128, 384), 0)
    group = lax.broadcasted_iota(jnp.int32, (128, 384), 1) // 32
    for a in range(3):
        pick = one_hot(128, 32, lambda row, lane: (lane == 9 * a + 3 * (row // 42) + row % 3) & (row < 126)).astype(BF)
        value = jnp.where(group == (row % 42) // 3 - a, dot(pick, colors), value)
    w1_ref[...] = value.astype(BF)
    for b in range(3):
        blocks = tiled_blocks(wmid_ref, lambda a: 3 * a + b, eye[:, :256])
        for row_in in range(8):
            start = b * 256 + row_in * 32
            w2_ref[start : start + 32, :] = banded(blocks, row_in, 6)
        blocks = tiled_blocks(wout_ref, lambda a: 3 * a + b, eye[:, :128])
        for row_in in range(8):
            value = banded(blocks, row_in, 4)
            for q in range(2):
                start = (b + q) * 256 + row_in * 32
                w3_ref[start : start + 32, q * 128 : q * 128 + 128] = value
    w3_ref[0:256, 128:256] = jnp.zeros((256, 128), BF)
    w3_ref[768:1024, 0:128] = jnp.zeros((256, 128), BF)


def cost_weights_kernel(wa_ref, wb_ref, ca_ref, cb_ref):
    eye = one_hot(32, 256, lambda row, lane: row == lane % 32).astype(BF)
    blank = jnp.zeros((768, 128), BF)
    cb_ref[0, :, 128:256] = blank
    cb_ref[3, :, 0:128] = blank
    for plane in range(3):
        for e in range(3):
            blocks = tiled_blocks(wa_ref, lambda a: 9 * plane + 3 * a + e, eye)
            for row_in in range(8):
                start = e * 256 + row_in * 32
                ca_ref[plane, start : start + 32, :] = banded(blocks, row_in, 6)
            blocks = tiled_blocks(wb_ref, lambda a: 9 * plane + 3 * a + e, eye[:, :128])
            for row_in in range(8):
                start = e * 256 + row_in * 32
                value = banded(blocks, row_in, 4)
                cb_ref[plane, start : start + 32, 0:128] = value
                cb_ref[plane + 1, start : start + 32, 128:256] = value


def near(value, axis, step):
    count = lax.axis_size(axis)
    return lax.ppermute(value, axis, [(i, (i + step) % count) for i in range(count)])


def swap(value, axis, bit):
    count = lax.axis_size(axis)
    return lax.ppermute(value, axis, [(i, i ^ bit) for i in range(count)])


def shards(
    images,
    shifts,
    in_weight,
    norm_gain,
    norm_bias,
    mid_weight,
    out_weight,
    cost_weight_a,
    cost_weight_b,
):
    views, rows, colors, width = images.shape
    planes = shifts.shape[1]
    chan = in_weight.shape[2]
    count = lax.axis_size("rows")
    index = lax.axis_index("rows")
    core = index % 2
    total = views * width

    own = images.reshape(views, rows * colors, width)
    pair = swap(own, "rows", 1)
    upper = jnp.where(core == 0, own, pair)
    lower = jnp.where(core == 0, pair, own)
    both = jnp.concatenate([upper, lower], axis=1)
    halo = 5 * colors
    above = near(both[:, 2 * rows * colors - halo :], "rows", 2)
    below = near(both[:, :halo], "rows", -2)

    params = pltpu.CompilerParams(vmem_limit_bytes=60 * 1024 * 1024)

    colors_in = in_weight.transpose(0, 1, 3, 2).reshape(9 * colors, chan)
    colors_in = jnp.pad(colors_in, ((0, 32 - 9 * colors), (0, 0)))
    w1, w2, w3 = pl.pallas_call(
        small_weights_kernel,
        name="small_weights",
        out_shape=(
            jax.ShapeDtypeStruct((128, 384), BF),
            jax.ShapeDtypeStruct((768, 256), BF),
            jax.ShapeDtypeStruct((1024, 256), BF),
        ),
        in_specs=[VMEM] * 3,
        out_specs=(VMEM,) * 3,
        cost_estimate=pl.CostEstimate(flops=2000000, bytes_accessed=1000000, transcendentals=0),
    )(colors_in, mid_weight.reshape(9, chan, chan), out_weight.reshape(9, chan, chan))
    ca, cb = pl.pallas_call(
        cost_weights_kernel,
        name="cost_weights",
        out_shape=(jax.ShapeDtypeStruct((3, 768, 256), BF), jax.ShapeDtypeStruct((4, 768, 256), BF)),
        in_specs=[VMEM] * 2,
        out_specs=(VMEM,) * 2,
        cost_estimate=pl.CostEstimate(flops=2000000, bytes_accessed=3500000, transcendentals=0),
        compiler_params=params,
    )(cost_weight_a.reshape(27, chan, chan), cost_weight_b.reshape(27, chan, chan))

    patches, stats = pl.pallas_call(
        stats_kernel,
        name="stats",
        out_shape=(
            jax.ShapeDtypeStruct((total, 128), BF),
            jax.ShapeDtypeStruct((2 * views, 128), F32),
        ),
        in_specs=[VMEM] * 4,
        out_specs=(VMEM, VMEM),
        scratch_shapes=[
            pltpu.VMEM((4, 64, width), F32),
            pltpu.VMEM((4, 128, width), F32),
            pltpu.VMEM((total, 128), F32),
            pltpu.VMEM((total, 256), F32),
        ],
        compiler_params=params,
    )(both, above, below, w1)
    bit = 2
    while True:
        other = swap(stats, "rows", bit)
        if 2 * bit >= count:
            break
        stats = jnp.concatenate(merge(stats, other, views, rows * width * bit), axis=0)
        bit *= 2

    return pl.pallas_call(
        main_kernel,
        name="main",
        out_shape=jax.ShapeDtypeStruct((planes, rows, chan, width), BF),
        in_specs=[SMEM] + [VMEM] * 8 + [pl.BlockSpec(memory_space=pl.ANY)] * 2,
        out_specs=VMEM,
        scratch_shapes=[
            pltpu.VMEM((total + 2 * views, 384), BF),
            pltpu.VMEM((2, total + 2 * views, 256), BF),
            pltpu.VMEM((2 * total, 128), F32),
            pltpu.VMEM((2, 9, width + 2 * REACH, 128), F32),
            pltpu.VMEM((2, 9, width + 2 * REACH, 128), F32),
            pltpu.VMEM((4, width + 16, 256), F32),
            pltpu.VMEM((planes + 2, width, 768), BF),
            pltpu.VMEM((planes // 2 + 1, 2, width, 768), BF),
            pltpu.VMEM((3, 768, 256), BF),
            pltpu.VMEM((4, 768, 256), BF),
            pltpu.VMEM((8, 128), F32),
            pltpu.SemaphoreType.DMA((2,)),
        ],
        compiler_params=params,
    )(shifts, patches, stats, other, norm_gain[None], norm_bias[None], w1, w2, w3, ca, cb)


def solution(mesh):
    placed = (P("groups", "rows", None, None), P("groups", None), P(), P(), P(), P(), P(), P(), P())
    return jax.shard_map(
        shards,
        mesh=mesh,
        in_specs=placed,
        out_specs=P("groups", "rows", None, None),
        check_vma=False,
    )
```

time: 135 us -> 63.1 us (0.47)
  local copies, waits for them, and re-layouts: 49.1 us -> 3.52 us
  matrix products: 13.8 us -> 0 us
  Pallas kernels: 47.4 us -> 37.2 us
  other arithmetic: 4.32 us -> 1.59 us
  waiting for transfers between devices: 12.1 us -> 13.7 us
    transpose x5 -> x0, local copies, waits for them, and re-layouts: 20.2 us -> none  [the longest x1 9.02 us: shards(): jnp.einsum('dbqcro,dps->pbqcsro', cb, plane_band())]
    reshape x5 -> x1, local copies, waits for them, and re-layouts: 19.5 us -> 0.72 us  [shards(): colors_in = in_weight.transpose(0, 1, 3, 2).reshape(9 * colors, chan)]
    dot_general x6 -> x0, matrix products: 13.8 us -> none  [the longest x1 5.21 us: shards(): jnp.einsum('dbqcro,dps->pbqcsro', cb, plane_band())]
    pallas_call x2 -> x3, Pallas kernels: 39.9 us -> 31.4 us  [the longest x1 25.9 us: shards(): pl.pallas_call(main_kernel, name='main', out_shape=jax.ShapeDtypeStruct((...]
    dot_general x1 -> x0, local copies, waits for them, and re-layouts: 5.09 us -> none  [shards(): cb = jnp.einsum('daboc,aqr->dbqcro', cost_weight_b, band(8, 4, 4))]
    ppermute x5 -> x4, waiting for transfers between devices: 6.79 us -> 10.2 us  [swap(): return lax.ppermute(value, axis, [(i, i ^ bit) for i in range(count)])]
    ppermute x2, waiting for transfers between devices: 5.36 us -> 3.54 us  [near(): lax.ppermute(value, axis, [(i, (i + step) % count) for i in range(count)])]
    pallas_call x1, Pallas kernels: 7.47 us -> 5.79 us  [shards(): pl.pallas_call(stats_kernel, name='stats', out_shape=(jax.ShapeDtypeStruc...]
  transfers between devices with their start and end apart: 7 -> 6, of which waited for: 5 -> 5; matrix products, arithmetic and copies ran while one was open for 46% -> 3% of each run, Pallas kernels for 0% -> 9%
where the time goes in v1:
time: 63.1 us; the launch traced here: 62.7 us
  Pallas kernels  37.2 us (59%)
  waiting for transfers between devices  13.7 us (22%)
  starting transfers between devices  6.63 us (11%)
  local copies, waits for them, and re-layouts  3.52 us (6%)
  other arithmetic  1.59 us (3%)
    pallas_call x1, Pallas kernels, shards(): pl.pallas_call(main_kernel, name='main', out_shape=jax.ShapeDtypeStruct((...  25.9 us
    ppermute x4, waiting for transfers between devices, swap(): return lax.ppermute(value, axis, [(i, i ^ bit) for i in range(count)])  10.2 us
    ppermute x2, starting transfers between devices, near(): lax.ppermute(value, axis, [(i, (i + step) % count) for i in range(count)])  5.97 us
    pallas_call x1, Pallas kernels, shards(): pl.pallas_call(stats_kernel, name='stats', out_shape=(jax.ShapeDtypeStruc...  5.79 us
    ppermute x2, waiting for transfers between devices, near(): lax.ppermute(value, axis, [(i, (i + step) % count) for i in range(count)])  3.54 us
    pallas_call x1, Pallas kernels, shards(): pl.pallas_call(cost_weights_kernel, name='cost_weights', out_shape=(jax.S...  3.1 us
    pallas_call x1, Pallas kernels, shards(): pl.pallas_call(small_weights_kernel, name='small_weights', out_shape=(jax...  2.37 us
    unnamed x9, local copies, waits for them, and re-layouts  2.16 us
  transfers between devices with their start and end apart: 6, of which 5 were waited for; matrix products, arithmetic and copies ran while one was open for 3% of the time, Pallas kernels for 9%

profile of v1, /device:TPU:0, one launch (start us, length us, event | category | flops | bytes accessed | tf_op | source)
XLA Modules:
  0.0 62.7 jit_solution(9188301960985907263)
XLA Ops:
  0.0 0.9 %copy.11 = bf16[16,4,3,256]{3,0,2,1:T(8,128)(2,1)S(1)} copy(bf16[16,4,3,256]{3,1,2,0:T(4,128)(2,1)} %param.9) | data formatting | bytes 196608 | tf_op args[0]
  0.9 0.5 collective-permute-start
  1.5 1.0 %collective-permute-done = bf16[16,12,256]{2,1,0:T(8,128)(2,1)S(1)} collective-permute-done((bf16[16,12,256]{2,1,0:T(8,128)(2,1)S(1)}, bf16[16,12,256]{2,1,0:T(8,128)(2,1)S(1)}, u32[]{:S(2)}, u32[]{:S(2)}) %collective-permute-start) | collective-permute-done | bytes 98336 | tf_op jit(solution)/shard_map/ppermute | solution.py:315
  2.5 0.1 fusion.1
  2.6 6.0 %collective-permute-start.2 = (bf16[16,15,256]{2,1,0:T(8,128)(2,1)S(1)}, bf16[16,15,256]{2,1,0:T(8,128)(2,1)S(1)}, u32[]{:S(2)}, u32[]{:S(2)}) collective-permute-start(bf16[16,15,256]{2,1,0:T(8,128)(2,1)S(1)} %get-tuple-element.19), channel_id=1, source_target_pairs={{0,14},{1,15},{2,0},{3,1},{4,2},{5,3},{6,4},{7,5},{8,6},{9,7},{10,... | collective-permute-start | bytes 368648 | tf_op jit(solution)/shard_map/ppermute | solution.py:310
  8.6 0.0 collective-permute-start.1
  8.6 0.7 %reshape.19 = bf16[27,32]{1,0:T(8,128)(2,1)S(1)} reshape(bf16[3,3,3,32]{3,2,1,0:T(4,128)(2,1)} %bitcast.14) | data formatting | bytes 3456 | tf_op jit(solution)/shard_map/reshape | solution.py:348
  9.3 0.6 pad.4.win_ref
  9.9 2.4 %small_weights.1 = (bf16[128,384]{1,0:T(8,128)(2,1)}, bf16[768,256]{1,0:T(8,128)(2,1)}, bf16[1024,256]{1,0:T(8,128)(2,1)}) custom-call(bf16[32,32]{1,0:T(8,128)(2,1)} %pad.4.win_ref, bf16[9,32,32]{2,1,0:T(8,128)(2,1)} %bitcast.12, bf16[9,32,32]{2,1,0:T(8,128)(2,1)} %bitcast.13), custom_call_target="tpu_custom_call" | custom-call | flops 2000000 | bytes 1000000 | tf_op jit(solution)/shard_map/small_weights/pallas_call | solution.py:350
  12.3 0.7 %pad_maximum_fusion.both_ref = bf16[16,24,256]{2,1,0:T(8,128)(2,1)} fusion(bf16[16,12,256]{2,1,0:T(8,128)(2,1)S(1)} %get-tuple-element.22, bf16[16,12,256]{2,1,0:T(8,128)(2,1)S(1)} %get-tuple-element.21), kind=kLoop, calls=%fused_computation.2 | loop fusion | flops 393216 | bytes 393216 | tf_op jit(solution)/shard_map/concatenate | solution.py:341
  13.0 0.0 collective-permute-done.2.below_ref
  13.0 0.0 copy-start
  13.0 3.5 %collective-permute-done.1.above_ref = bf16[16,15,256]{2,1,0:T(8,128)(2,1)S(1)} collective-permute-done((bf16[16,15,256]{2,1,0:T(8,128)(2,1)S(1)}, bf16[16,15,256]{2,1,0:T(8,128)(2,1)S(1)}, u32[]{:S(2)}, u32[]{:S(2)}) %collective-permute-start.1) | collective-permute-done | bytes 122912 | tf_op jit(solution)/shard_map/ppermute | solution.py:310
  16.5 0.0 copy-start.1
  16.5 0.0 copy-done
  16.5 0.7 %copy-done.1 = bf16[16,15,256]{2,1,0:T(8,128)(2,1)} copy-done((bf16[16,15,256]{2,1,0:T(8,128)(2,1)}, bf16[16,15,256]{2,1,0:T(8,128)(2,1)S(1)}, u32[]{:S(2)}) %copy-start.1) | copy-done | bytes 122904
  17.2 5.8 %stats.1 = (bf16[4096,128]{1,0:T(8,128)(2,1)}, f32[32,128]{1,0:T(8,128)}) custom-call(bf16[16,24,256]{2,1,0:T(8,128)(2,1)} %pad_maximum_fusion.both_ref, bf16[16,15,256]{2,1,0:T(8,128)(2,1)} %copy-done.1, bf16[16,15,256]{2,1,0:T(8,128)(2,1)} %copy-done, bf16[128,384]{1,0:T(8,128)(2,1)} %get-tuple-element.12.w_ref.w1_ref), custom_call_target="tpu_custom_call" | custom-call | tf_op jit(solution)/shard_map/stats/pallas_call | solution.py:372
  23.0 0.0 collective-permute-start.3
  23.0 3.9 %collective-permute-done.3 = f32[32,128]{1,0:T(8,128)S(1)} collective-permute-done((f32[32,128]{1,0:T(8,128)}, f32[32,128]{1,0:T(8,128)S(1)}, u32[]{:S(2)}, u32[]{:S(2)}) %collective-permute-start.3) | collective-permute-done | bytes 16416 | tf_op jit(solution)/shard_map/ppermute | solution.py:315
  26.9 0.7 %add_multiply_fusion.1 = (f32[16,128]{1,0:T(8,128)S(1)}, f32[16,128]{1,0:T(8,128)S(1)}) fusion(f32[32,128]{1,0:T(8,128)S(1)} %collective-permute-done.3, f32[32,128]{1,0:T(8,128)} %get-tuple-element.14), kind=kLoop, calls=%fused_computation.16 | loop fusion | flops 14336 | bytes 49152 | tf_op jit(solution)/shard_map/mul | solution.py:88
  27.6 0.1 collective-permute-start.4
  27.7 3.7 %collective-permute-done.4 = f32[32,128]{1,0:T(8,128)S(1)} collective-permute-done((f32[32,128]{1,0:T(8,128)S(1)}, f32[32,128]{1,0:T(8,128)S(1)}, u32[]{:S(2)}, u32[]{:S(2)}) %collective-permute-start.4) | collective-permute-done | bytes 16416 | tf_op jit(solution)/shard_map/ppermute | solution.py:315
  31.5 0.0 copy-start.2
  31.5 0.1 collective-permute-start.5
  31.5 3.1 %cost_weights.1 = (bf16[3,768,256]{2,1,0:T(8,128)(2,1)}, bf16[4,768,256]{2,1,0:T(8,128)(2,1)}) custom-call(bf16[27,32,32]{2,1,0:T(8,128)(2,1)} %bitcast.10, bf16[27,32,32]{2,1,0:T(8,128)(2,1)} %bitcast.11), custom_call_target="tpu_custom_call" | custom-call | flops 2000000 | bytes 3500000 | tf_op jit(solution)/shard_map/cost_weights/pallas_call | solution.py:362
  34.6 1.5 %collective-permute-done.5.other_ref = f32[32,128]{1,0:T(8,128)S(1)} collective-permute-done((f32[32,128]{1,0:T(8,128)S(1)}, f32[32,128]{1,0:T(8,128)S(1)}, u32[]{:S(2)}, u32[]{:S(2)}) %collective-permute-start.5) | collective-permute-done | bytes 16416 | tf_op jit(solution)/shard_map/ppermute | solution.py:315
  36.2 0.0 copy-start.3
  36.2 0.0 copy-done.2
  36.2 0.6 copy-done.3
  36.8 25.9 %main.1 = bf16[12,4,32,256]{3,2,1,0:T(8,128)(2,1)} custom-call(s32[16,12]{1,0:T(8,128)} %shifts.1, bf16[4096,128]{1,0:T(8,128)(2,1)} %get-tuple-element.13.pt_ref, f32[32,128]{1,0:T(8,128)} %copy-done.2, f32[32,128]{1,0:T(8,128)} %copy-done.3, f32[1,32]{1,0:T(1,128)} %bitcast.15, f32[1,32]{1,0:T(1,128)} %bitcast.16, ...), custom_call_target="tpu_custom_call" | custom-call | tf_op jit(solution)/shard_map/main/pallas_call | solution.py:397
  (5 shorter events, 0.1 us)
Async XLA Ops:
  0.9 1.5 %collective-permute-start = (bf16[16,12,256]{2,1,0:T(8,128)(2,1)S(1)}, bf16[16,12,256]{2,1,0:T(8,128)(2,1)S(1)}, u32[]{:S(2)}, u32[]{:S(2)}) collective-permute-start(bf16[16,12,256]{2,1,0:T(8,128)(2,1)S(1)} %copy.13), channel_id=1, source_target_pairs={{0,1},{1,0},{2,3},{3,2},{4,5},{5,4},{6,7},{7,6},{8,9},{9,8},{10,11... | collective-permute-start | bytes 294920 | tf_op jit(solution)/shard_map/ppermute | solution.py:315
  2.6 10.4 %collective-permute-start.2 = (bf16[16,15,256]{2,1,0:T(8,128)(2,1)S(1)}, bf16[16,15,256]{2,1,0:T(8,128)(2,1)S(1)}, u32[]{:S(2)}, u32[]{:S(2)}) collective-permute-start(bf16[16,15,256]{2,1,0:T(8,128)(2,1)S(1)} %get-tuple-element.19), channel_id=1, source_target_pairs={{0,14},{1,15},{2,0},{3,1},{4,2},{5,3},{6,4},{7,5},{8,6},{9,7},{10,... | collective-permute-start | bytes 368648 | tf_op jit(solution)/shard_map/ppermute | solution.py:310
  8.6 8.0 %collective-permute-start.1 = (bf16[16,15,256]{2,1,0:T(8,128)(2,1)S(1)}, bf16[16,15,256]{2,1,0:T(8,128)(2,1)S(1)}, u32[]{:S(2)}, u32[]{:S(2)}) collective-permute-start(bf16[16,15,256]{2,1,0:T(8,128)(2,1)S(1)} %get-tuple-element.20), channel_id=1, source_target_pairs={{0,2},{1,3},{2,4},{3,5},{4,6},{5,7},{6,8},{7,9},{8,10},{9,11},{10,... | collective-permute-start | bytes 368648 | tf_op jit(solution)/shard_map/ppermute | solution.py:310
  13.0 3.5 %copy-start = (bf16[16,15,256]{2,1,0:T(8,128)(2,1)}, bf16[16,15,256]{2,1,0:T(8,128)(2,1)S(1)}, u32[]{:S(2)}) copy-start(bf16[16,15,256]{2,1,0:T(8,128)(2,1)S(1)} %collective-permute-done.2.below_ref) | copy-start | bytes 368644
  16.5 0.7 %copy-start.1 = (bf16[16,15,256]{2,1,0:T(8,128)(2,1)}, bf16[16,15,256]{2,1,0:T(8,128)(2,1)S(1)}, u32[]{:S(2)}) copy-start(bf16[16,15,256]{2,1,0:T(8,128)(2,1)S(1)} %collective-permute-done.1.above_ref) | copy-start | bytes 368644
  23.0 3.9 %collective-permute-start.3 = (f32[32,128]{1,0:T(8,128)}, f32[32,128]{1,0:T(8,128)S(1)}, u32[]{:S(2)}, u32[]{:S(2)}) collective-permute-start(f32[32,128]{1,0:T(8,128)} %get-tuple-element.14), channel_id=1, source_target_pairs={{0,2},{1,3},{2,0},{3,1},{4,6},{5,7},{6,4},{7,5},{8,10},{9,11},{10,... | collective-permute-start | bytes 49160 | tf_op jit(solution)/shard_map/ppermute | solution.py:315
  27.6 3.8 %collective-permute-start.4 = (f32[32,128]{1,0:T(8,128)S(1)}, f32[32,128]{1,0:T(8,128)S(1)}, u32[]{:S(2)}, u32[]{:S(2)}) collective-permute-start(f32[32,128]{1,0:T(8,128)S(1)} %pad_maximum_fusion.1), channel_id=1, source_target_pairs={{0,4},{1,5},{2,6},{3,7},{4,0},{5,1},{6,2},{7,3},{8,12},{9,13},{10,... | collective-permute-start | bytes 49160 | tf_op jit(solution)/shard_map/ppermute | solution.py:315
  31.5 4.7 %copy-start.2 = (f32[32,128]{1,0:T(8,128)}, f32[32,128]{1,0:T(8,128)S(1)}, u32[]{:S(2)}) copy-start(f32[32,128]{1,0:T(8,128)S(1)} %pad_maximum_fusion.2.st_ref) | copy-start | bytes 49156
  31.5 4.7 %collective-permute-start.5 = (f32[32,128]{1,0:T(8,128)S(1)}, f32[32,128]{1,0:T(8,128)S(1)}, u32[]{:S(2)}, u32[]{:S(2)}) collective-permute-start(f32[32,128]{1,0:T(8,128)S(1)} %pad_maximum_fusion.2.st_ref), channel_id=1, source_target_pairs={{0,8},{1,9},{2,10},{3,11},{4,12},{5,13},{6,14},{7,15},{8,0},{9,1},... | collective-permute-start | bytes 49160 | tf_op jit(solution)/shard_map/ppermute | solution.py:315
  36.2 0.6 copy-start.3

commit v2 on v1

v2 whole, which is shorter than its diff:
```python
import functools
import jax
import jax.numpy as jnp
import numpy as np
from jax import lax
from jax.experimental import pallas as pl
from jax.experimental.pallas import tpu as pltpu
from jax.sharding import PartitionSpec as P

BF = jnp.bfloat16
F32 = jnp.float32
VMEM = pl.BlockSpec(memory_space=pltpu.VMEM)
SMEM = pl.BlockSpec(memory_space=pltpu.SMEM)
REACH = 48


def dot(a, b):
    return jnp.dot(a, b, preferred_element_type=F32)


def fold(sums):
    sums = sums + pltpu.roll(sums, 64, 1)
    return sums + pltpu.roll(sums, 32, 1)


def stats_kernel(own_ref, pair_ref, far_ref, near_ref, next_ref, w_ref, pt_ref, st_ref, x_scr, p_scr, t_scr):
    views, tall, width = own_ref.shape
    index = lax.axis_index("rows")
    first_core = index % 2 == 0
    top = (index >= 2).astype(F32)
    bottom = (index < lax.axis_size("rows") - 2).astype(F32)
    beyond = jnp.where(first_core, top, bottom)
    lane = lax.broadcasted_iota(jnp.int32, (1, width), 1)
    p_scr[...] = jnp.zeros_like(p_scr)
    slots = p_scr.shape[0]

    def some_views(i, carry):
        for slot in range(slots):
            v = i * slots + slot
            pair = pair_ref[v].astype(F32)
            far = far_ref[v].astype(F32) * beyond
            one = near_ref[v].astype(F32)
            two = next_ref[v].astype(F32)
            x_scr[slot, 0:3, :] = jnp.where(first_core, one, two) * top
            x_scr[slot, 3:15, :] = jnp.where(first_core, far, pair)
            x_scr[slot, 15:27, :] = own_ref[v].astype(F32)
            x_scr[slot, 27:39, :] = jnp.where(first_core, pair, far)
            x_scr[slot, 39:42, :] = jnp.where(first_core, two, one) * bottom
            x = x_scr[slot, 0:42, :]
            p_scr[slot, 0:42, :] = jnp.where(lane == 0, 0.0, pltpu.roll(x, 1, 1))
            p_scr[slot, 42:84, :] = x
            p_scr[slot, 84:126, :] = jnp.where(lane == width - 1, 0.0, pltpu.roll(x, width - 1, 1))
            t_scr[pl.ds(v, width, stride=views), :] = p_scr[slot].T
        return carry

    lax.fori_loop(0, views // slots, some_views, 0)
    chunk = 1024
    steps = views * width // chunk
    weight = w_ref[:, pl.ds(pl.multiple_of(jnp.where(first_core, 128, 0), 128), 256)]
    center = None
    total = squares = 0.0
    for i in range(steps):
        rows = slice(i * chunk, (i + 1) * chunk)
        patch = t_scr[rows, :].astype(BF)
        pt_ref[rows, :] = patch
        raw = dot(patch, weight).reshape(chunk // views, views, 256)
        if center is None:
            start = jnp.sum(raw, axis=0)
            center = fold(start[:, :128] + start[:, 128:]) * (1.0 / (8 * chunk // views))
        for half in range(2):
            part = raw[:, :, half * 128 : half * 128 + 128] - center[None]
            total = total + jnp.sum(part, axis=0)
            squares = squares + jnp.sum(part * part, axis=0)
    offset = fold(total) * (1.0 / (8 * width))
    st_ref[0:views, :] = center + offset
    st_ref[views:, :] = fold(squares) - offset * offset * (8.0 * width)


def row_mask(first, lanes):
    row = lax.axis_index("rows") * 4 + first + (lax.broadcasted_iota(jnp.int32, (1, lanes), 1) >> 5)
    return jnp.where((row >= 0) & (row < lax.axis_size("rows") * 4), 1.0, 0.0).astype(F32)


def merge(one, two, views, cells):
    gap = one[:views] - two[:views]
    mean = (one[:views] + two[:views]) * 0.5
    return mean, one[views:] + two[views:] + gap * gap * (0.5 * cells)


def tiled_lanes(scr, ref):
    scr[...] = jnp.zeros_like(scr)
    scr[0:1, 0:32] = ref[...]
    return fold(scr[...])[0:1]


def main_kernel(
    shifts, pt_ref, st_ref, other_ref, gain_ref, bias_ref, w1_ref, w2_ref, w3_ref, ca_hbm, cb_hbm, out_ref,
    nb, mid, f_scr, s_low, s_high, q_low, q_high, v32, vb, hb, ca_ref, cb_ref, g_scr, sems,
):
    copies = [
        pltpu.make_async_copy(ca_hbm, ca_ref, sems.at[0]),
        pltpu.make_async_copy(cb_hbm, cb_ref, sems.at[1]),
    ]
    for copy in copies:
        copy.start()
    s_scr, q_scr = (s_low, s_high), (q_low, q_high)
    views = st_ref.shape[0] // 2
    total = pt_ref.shape[0]
    planes = out_ref.shape[0]
    width = out_ref.shape[3]
    cells = lax.axis_size("rows") * 4 * width
    mean, squares = merge(st_ref[...], other_ref[...], views, cells // 2)
    scale = tiled_lanes(g_scr, gain_ref) / jnp.sqrt(squares * (1.0 / cells) + 1e-05)
    shift = tiled_lanes(g_scr, bias_ref)
    edge = jnp.zeros((views, 384), BF)
    nb[0:views, :] = edge
    nb[views + total :, :] = edge
    for block in range(2):
        mid[block, 0:views, :] = edge[:, :256]
        mid[block, views + total :, :] = edge[:, :256]
    size = 1024
    cols = size // views
    steps = total // size
    masks = [row_mask(4 * group - 4, 128) for group in range(3)]

    def normalize(i, carry):
        rows = pl.ds(pl.multiple_of(i * size, size), size)
        out = pl.ds(pl.multiple_of(i * size + views, views), size)
        raw = dot(pt_ref[rows, :], w1_ref[...])
        for group in range(3):
            part = raw[:, group * 128 : group * 128 + 128].reshape(cols, views, 128)
            part = jnp.maximum((part - mean[None]) * scale[None] + shift[None], 0.0) * masks[group][None]
            nb[out, group * 128 : group * 128 + 128] = part.reshape(size, 128).astype(BF)
        return carry

    mid_masks = [row_mask(4 * block - 3, 256) for block in range(2)]

    def middle(i, carry):
        out = pl.ds(pl.multiple_of(i * size + views, views), size)
        for block in range(2):
            taps = [
                nb[pl.ds(pl.multiple_of(i * size + b * views, views), size), block * 128 : block * 128 + 256]
                for b in range(3)
            ]
            part = dot(jnp.concatenate(taps, axis=1), w2_ref[...])
            part = jnp.maximum(part, 0.0) * mid_masks[block]
            mid[block, out, :] = part.astype(BF)
        return carry

    last_masks = [row_mask(4 * block - 2, 128) for block in range(2)]
    couples = 32
    apart = 17

    def last(i, carry):
        for block in range(2):
            rows = pl.ds(i * couples * 2 * views, (couples + 1) * 2 * views)
            value = mid[block, rows, :].reshape(couples + 1, 2, views, 256)
            taps = [value[j // 2 : j // 2 + couples, j % 2].reshape(couples * views, 256) for j in range(4)]
            part = dot(jnp.concatenate(taps, axis=1), w3_ref[...])
            for q in range(2):
                half = (part[:, q * 128 : q * 128 + 128] * last_masks[block]).astype(BF).astype(F32)
                for m in range(couples):
                    start = (block * width + (i * couples + m) * 2 + q) * apart
                    f_scr[start : start + views, :] = half[m * views : (m + 1) * views]

    for ref in s_scr + q_scr:
        ref[...] = jnp.zeros_like(ref)

    def add_views(i):
        for v in range(views):
            step = shifts[v, 0] + 4
            for block in range(2):
                feats = f_scr[pl.ds((block * width + i * cols) * apart + v, cols, stride=apart), :]
                s_scr[block][step, REACH + i * cols : REACH + (i + 1) * cols, :] += feats
                q_scr[block][step, REACH + i * cols : REACH + (i + 1) * cols, :] += feats * feats

    for i in range(steps + 3):
        if i < steps:
            normalize(i, 0)
        if 0 <= i - 1 < steps:
            middle(i - 1, 0)
        if 0 <= i - 2 < steps:
            last(i - 2, 0)
        if 0 <= i - 3 < steps:
            add_views(i - 3)

    for pair in (0, planes // 2):
        hb[pair, pair * 2 // planes] = jnp.zeros_like(hb[0, 0])
    vb[0] = jnp.zeros_like(vb[0])
    vb[planes + 1] = jnp.zeros_like(vb[0])
    v32[...] = jnp.zeros_like(v32)

    part_size = 32

    def one_plane(k, carry):
        for block in range(2):
            for part in range(width // part_size):
                start = REACH + part * part_size
                summed = s_scr[block][4, start : start + part_size, :]
                squares = q_scr[block][4, start : start + part_size, :]
                for step in (-4, -3, -2, -1, 1, 2, 3, 4):
                    rows = pl.ds(start + step * (k + 1), part_size)
                    summed = summed + s_scr[block][step + 4, rows, :]
                    squares = squares + q_scr[block][step + 4, rows, :]
                average = summed * (1.0 / views)
                value = (squares * (1.0 / views) - average * average).astype(BF)
                v32[k % 4, 8 + part * part_size : 8 + part * part_size + part_size, block * 128 : block * 128 + 128] = (
                    value.astype(F32)
                )
        for tap in range(3):
            vb[k + 1, :, tap * 256 : tap * 256 + 256] = v32[k % 4, 7 + tap : 7 + tap + width, :].astype(BF)
        return carry

    mask = row_mask(-1, 256)
    group = 2

    def hidden(i, carry):
        k = i * group
        value = dot(jnp.concatenate([vb[pl.ds(k + d, group)].reshape(group * width, 768) for d in range(3)], axis=1), ca_ref[...].reshape(2304, 256))
        value = (jnp.maximum(value, 0.0) * mask).astype(BF).astype(F32)
        for t in range(group):
            v32[4 + 2 * (i % 2) + t, 8 : 8 + width, :] = value[t * width : (t + 1) * width]
            plane = k + t + 1
            for tap in range(3):
                hb[plane // 2, plane % 2, :, tap * 256 : tap * 256 + 256] = v32[4 + 2 * (i % 2) + t, 7 + tap : 7 + tap + width, :].astype(BF)
        return carry

    pairs = 3

    def final(i, carry):
        j = i * pairs
        taps = [hb[pl.ds(j + p // 2, pairs), p % 2].reshape(pairs * width, 768) for p in range(4)]
        value = dot(jnp.concatenate(taps, axis=1), cb_ref[...].reshape(3072, 256))
        for t in range(pairs):
            part = value[t * width : (t + 1) * width].T
            out_ref[pl.ds(2 * (j + t), 2)] = part.astype(BF).reshape(2, 4, 32, width)
        return carry

    for copy in copies:
        copy.wait()
    for k in range(4):
        one_plane(k, 0)
    for i in range(6):
        hidden(i, 0)
        if i < 4:
            one_plane(2 * i + 4, 0)
            one_plane(2 * i + 5, 0)
    final(0, 0)
    final(1, 0)


def one_hot(rows, lanes, same):
    row = lax.broadcasted_iota(jnp.int32, (rows, lanes), 0)
    lane = lax.broadcasted_iota(jnp.int32, (rows, lanes), 1)
    return jnp.where(same(row, lane), 1.0, 0.0)


def tiled_blocks(w_ref, index, eye):
    return [
        lax.dot_general(w_ref[index(a)], eye, (((0,), (0,)), ((), ())), preferred_element_type=F32) for a in range(3)
    ]


def banded(blocks, row_in, used):
    group = lax.broadcasted_iota(jnp.int32, blocks[0].shape, 1) >> 5
    value = jnp.zeros_like(blocks[0])
    for a in range(3):
        if 0 <= row_in - a < used:
            value = jnp.where(group == row_in - a, blocks[a], value)
    return value.astype(BF)


def color_weights_kernel(w_ref, pick_ref, tap_ref, w1_ref):
    eye = one_hot(32, 384, lambda row, lane: row == (lane & 31)).astype(BF)
    colors = dot(w_ref[...], eye).astype(BF)
    picked = dot(pick_ref[...], colors)
    taps = tap_ref[...]
    value = jnp.zeros((128, 384), F32)
    for a in range(3):
        value = jnp.where(taps == a, picked[a * 128 : a * 128 + 128], value)
    w1_ref[...] = value.astype(BF)


def color_places(rows_in, rows_out):
    pick = np.zeros((3, 128, 27), np.float32)
    taps = np.full((128, rows_out, 32), 3, np.int32)
    for b in range(3):
        for row in range(rows_in):
            for c in range(3):
                place = (b * rows_in + row) * 3 + c
                for a in range(3):
                    pick[a, place, 9 * a + 3 * b + c] = 1.0
                    if 0 <= row - a < rows_out:
                        taps[place, row - a] = a
    return jnp.asarray(pick.reshape(384, 27), BF), jnp.asarray(taps.reshape(128, rows_out * 32))


def feature_weights_kernel(wmid_ref, wout_ref, w2_ref, w3_ref):
    eye = one_hot(32, 256, lambda row, lane: row == (lane & 31)).astype(BF)
    for b in range(3):
        blocks = tiled_blocks(wmid_ref, lambda a: 3 * a + b, eye)
        for row_in in range(8):
            start = b * 256 + row_in * 32
            w2_ref[start : start + 32, :] = banded(blocks, row_in, 6)
        blocks = tiled_blocks(wout_ref, lambda a: 3 * a + b, eye[:, :128])
        for row_in in range(8):
            value = banded(blocks, row_in, 4)
            for q in range(2):
                start = (b + q) * 256 + row_in * 32
                w3_ref[start : start + 32, q * 128 : q * 128 + 128] = value
    w3_ref[0:256, 128:256] = jnp.zeros((256, 128), BF)
    w3_ref[768:1024, 0:128] = jnp.zeros((256, 128), BF)


def hidden_weights_kernel(w_ref, ca_ref):
    eye = one_hot(32, 256, lambda row, lane: row == (lane & 31)).astype(BF)
    for plane in range(3):
        for e in range(3):
            blocks = tiled_blocks(w_ref, lambda a: 9 * plane + 3 * a + e, eye)
            for row_in in range(8):
                start = e * 256 + row_in * 32
                ca_ref[plane, start : start + 32, :] = banded(blocks, row_in, 6)


def final_weights_kernel(w_ref, cb_ref):
    eye = one_hot(32, 128, lambda row, lane: row == (lane & 31)).astype(BF)
    blank = jnp.zeros((768, 128), BF)
    cb_ref[0, :, 128:256] = blank
    cb_ref[3, :, 0:128] = blank
    for plane in range(3):
        for e in range(3):
            blocks = tiled_blocks(w_ref, lambda a: 9 * plane + 3 * a + e, eye)
            for row_in in range(8):
                start = e * 256 + row_in * 32
                value = banded(blocks, row_in, 4)
                cb_ref[plane, start : start + 32, 0:128] = value
                cb_ref[plane + 1, start : start + 32, 128:256] = value


def send(value, axis, even, odd):
    count = lax.axis_size(axis)
    pairs = []
    for i in range(count):
        to = i + (odd if i % 2 else even)
        if not 0 <= to < count:
            to = i ^ 1 if abs(even) == 2 else i
        pairs.append((i, to))
    return lax.ppermute(value, axis, pairs)


def swap(value, axis, bit):
    count = lax.axis_size(axis)
    return lax.ppermute(value, axis, [(i, i ^ bit) for i in range(count)])


def limit(mib):
    return pltpu.CompilerParams(vmem_limit_bytes=mib * 1024 * 1024)


def shards(
    images,
    shifts,
    in_weight,
    norm_gain,
    norm_bias,
    mid_weight,
    out_weight,
    cost_weight_a,
    cost_weight_b,
):
    views, rows, colors, width = images.shape
    planes = shifts.shape[1]
    chan = in_weight.shape[2]
    count = lax.axis_size("rows")
    index = lax.axis_index("rows")
    core = index % 2
    total = views * width


    def weights(kernel, shapes, *operands):
        shapes = tuple(jax.ShapeDtypeStruct(shape, BF) for shape in shapes)
        size = 2 * sum(shape.size for shape in shapes)
        return pl.pallas_call(
            kernel,
            name=kernel.__name__,
            out_shape=shapes,
            in_specs=[VMEM] * len(operands),
            out_specs=(VMEM,) * len(shapes),
            cost_estimate=pl.CostEstimate(flops=size, bytes_accessed=2 * size, transcendentals=0),
            compiler_params=limit(8),
        )(*operands)

    own = images.reshape(views, rows * colors, width)
    head, tail = own[:, :colors], own[:, (rows - 1) * colors :]
    pair = swap(own, "rows", 1)
    far = send(own, "rows", -1, 1)
    near = send(jnp.where(core == 0, tail, head), "rows", 2, -2)
    after = send(jnp.where(core == 0, head, tail), "rows", -2, 2)
    colors_in = in_weight.transpose(0, 1, 3, 2).reshape(9 * colors, chan)
    (w1,) = weights(color_weights_kernel, [(128, 384)], colors_in, *color_places(rows + 10, rows + 8))

    patches, stats = pl.pallas_call(
        stats_kernel,
        name="stats",
        out_shape=(
            jax.ShapeDtypeStruct((total, 128), BF),
            jax.ShapeDtypeStruct((2 * views, 128), F32),
        ),
        in_specs=[VMEM] * 6,
        out_specs=(VMEM, VMEM),
        scratch_shapes=[
            pltpu.VMEM((4, 48, width), F32),
            pltpu.VMEM((4, 128, width), F32),
            pltpu.VMEM((total, 128), F32),
        ],
        compiler_params=limit(12),
    )(own, pair, far, near, after, w1)
    jobs = [
        (feature_weights_kernel, [(768, 256), (1024, 256)], (mid_weight.reshape(9, chan, chan), out_weight.reshape(9, chan, chan))),
        (hidden_weights_kernel, [(3, 768, 256)], (cost_weight_a.reshape(27, chan, chan),)),
        (final_weights_kernel, [(4, 768, 256)], (cost_weight_b.reshape(27, chan, chan),)),
    ]
    made = []
    bit = 2
    while True:
        last = 2 * bit >= count
        other = swap(stats, "rows", bit)
        while jobs:
            kernel, shapes, operands = jobs.pop(0)
            stats, operands = lax.optimization_barrier((stats, operands))
            new = weights(kernel, shapes, *operands)
            if not last:
                other, new = lax.optimization_barrier((other, new))
            made.extend(new)
            if not last:
                break
        if last:
            break
        stats = jnp.concatenate(merge(stats, other, views, rows * width * bit), axis=0)
        bit *= 2
    w2, w3, ca, cb = made

    return pl.pallas_call(
        main_kernel,
        name="main",
        out_shape=jax.ShapeDtypeStruct((planes, rows, chan, width), BF),
        in_specs=[SMEM] + [VMEM] * 8 + [pl.BlockSpec(memory_space=pl.ANY)] * 2,
        out_specs=VMEM,
        scratch_shapes=[
            pltpu.VMEM((total + 2 * views, 384), BF),
            pltpu.VMEM((2, total + 2 * views, 256), BF),
            pltpu.VMEM((2 * width * 17, 128), F32),
            *[pltpu.VMEM((9, width + 2 * REACH, 128), F32) for _ in range(4)],
            pltpu.VMEM((8, width + 16, 256), F32),
            pltpu.VMEM((planes + 2, width, 768), BF),
            pltpu.VMEM((planes // 2 + 1, 2, width, 768), BF),
            pltpu.VMEM((3, 768, 256), BF),
            pltpu.VMEM((4, 768, 256), BF),
            pltpu.VMEM((8, 128), F32),
            pltpu.SemaphoreType.DMA((2,)),
        ],
        compiler_params=limit(44),
    )(shifts, patches, stats, other, norm_gain[None], norm_bias[None], w1, w2, w3, ca, cb)


def solution(mesh):
    placed = (P("groups", "rows", None, None), P("groups", None), P(), P(), P(), P(), P(), P(), P())
    return jax.shard_map(
        shards,
        mesh=mesh,
        in_specs=placed,
        out_specs=P("groups", "rows", None, None),
        check_vma=False,
    )
```

time: 63.1 us -> 47.5 us (0.75)
  Pallas kernels: 37.2 us -> 23.9 us
  waiting for transfers between devices: 13.7 us -> 4.12 us
  starting transfers between devices: 6.63 us -> 15.3 us
  other arithmetic: 1.59 us -> 0.06 us
    ppermute x4, starting transfers between devices: 0.66 us -> 12.4 us  [swap(): return lax.ppermute(value, axis, [(i, i ^ bit) for i in range(count)])]
    pallas_call x1, Pallas kernels: 25.9 us -> 18.9 us  [shards(): pl.pallas_call(main_kernel, name='main', out_shape=jax.ShapeDtypeStruct((...]
    ppermute x4, waiting for transfers between devices: 10.2 us -> 4.11 us  [swap(): return lax.ppermute(value, axis, [(i, i ^ bit) for i in range(count)])]
    pallas_call x2 -> x4, Pallas kernels: 5.47 us -> 1.33 us  [weights(): pl.pallas_call(kernel, name=kernel.__name__, out_shape=shapes, in_specs=[...]
    ppermute x2 -> x3, waiting for transfers between devices: 3.54 us -> 0.01 us  [send(): return lax.ppermute(value, axis, pairs)]
    ppermute x2 -> x3, starting transfers between devices: 5.97 us -> 2.88 us  [send(): return lax.ppermute(value, axis, pairs)]
    pallas_call x1, Pallas kernels: 5.79 us -> 3.71 us  [shards(): pl.pallas_call(stats_kernel, name='stats', out_shape=(jax.ShapeDtypeStruc...]
    concatenate x2 -> x0, other arithmetic: 0.81 us -> none  [shards(): both = jnp.concatenate([upper, lower], axis=1)]
  transfers between devices with their start and end apart: 6 -> 7, of which waited for: 5 -> 3; matrix products, arithmetic and copies ran while one was open for 3% -> 2% of each run, Pallas kernels for 9% -> 3%
where the time goes in v2:
time: 47.5 us; the launch traced here: 47.3 us
  Pallas kernels  23.9 us (50%)
  starting transfers between devices  15.3 us (32%)
  waiting for transfers between devices  4.12 us (9%)
  local copies, waits for them, and re-layouts  3.54 us (7%)
    pallas_call x1, Pallas kernels, shards(): pl.pallas_call(main_kernel, name='main', out_shape=jax.ShapeDtypeStruct((...  18.9 us
    ppermute x4, starting transfers between devices, swap(): return lax.ppermute(value, axis, [(i, i ^ bit) for i in range(count)])  12.4 us
    ppermute x4, waiting for transfers between devices, swap(): return lax.ppermute(value, axis, [(i, i ^ bit) for i in range(count)])  4.11 us
    pallas_call x1, Pallas kernels, shards(): pl.pallas_call(stats_kernel, name='stats', out_shape=(jax.ShapeDtypeStruc...  3.71 us
    ppermute x3, starting transfers between devices, send(): return lax.ppermute(value, axis, pairs)  2.88 us
    unnamed x19, local copies, waits for them, and re-layouts  2.79 us
    pallas_call x4, Pallas kernels, weights(): pl.pallas_call(kernel, name=kernel.__name__, out_shape=shapes, in_specs=[...  1.33 us
  transfers between devices with their start and end apart: 7, of which 3 were waited for; matrix products, arithmetic and copies ran while one was open for 2% of the time, Pallas kernels for 3%

profile of v2, /device:TPU:0, one launch (start us, length us, event | category | flops | bytes accessed | tf_op | source)
XLA Modules:
  0.0 47.3 jit_solution(17047926277591525571)
XLA Ops:
  0.0 1.0 %copy.13 = bf16[16,4,3,256]{3,0,2,1:T(8,128)(2,1)S(1)} copy(bf16[16,4,3,256]{3,1,2,0:T(4,128)(2,1)} %param.11) | data formatting | bytes 196608 | tf_op args[0]
  1.0 0.0 copy-start
  1.0 0.8 %collective-permute-start.1 = (bf16[16,12,256]{2,1,0:T(8,128)(2,1)S(1)}, bf16[16,12,256]{2,1,0:T(8,128)(2,1)S(1)}, u32[]{:S(2)}, u32[]{:S(2)}) collective-permute-start(bf16[16,12,256]{2,1,0:T(8,128)(2,1)S(1)} %copy.18.own_ref), channel_id=1, source_target_pairs={{0,0},{1,2},{2,1},{3,4},{4,3},{5,6},{6,5},{7,8},{8,7},{9,10},{10,9... | collective-permute-start | bytes 294920 | tf_op jit(solution)/shard_map/ppermute | solution.py:348
  1.8 4.4 %collective-permute-start = (bf16[16,12,256]{2,1,0:T(8,128)(2,1)S(1)}, bf16[16,12,256]{2,1,0:T(8,128)(2,1)S(1)}, u32[]{:S(2)}, u32[]{:S(2)}) collective-permute-start(bf16[16,12,256]{2,1,0:T(8,128)(2,1)S(1)} %copy.18.own_ref), channel_id=1, source_target_pairs={{0,1},{1,0},{2,3},{3,2},{4,5},{5,4},{6,7},{7,6},{8,9},{9,8},{10,11... | collective-permute-start | bytes 294920 | tf_op jit(solution)/shard_map/ppermute | solution.py:353
  6.3 0.1 collective-permute-start.3
  6.3 2.0 %collective-permute-start.2 = (bf16[16,3,256]{2,1,0:T(4,128)(2,1)S(1)}, bf16[16,3,256]{2,1,0:T(4,128)(2,1)S(1)}, u32[]{:S(2)}, u32[]{:S(2)}) collective-permute-start(bf16[16,3,256]{2,1,0:T(4,128)(2,1)S(1)} %get-tuple-element.38), channel_id=1, source_target_pairs={{0,2},{1,0},{2,4},{3,1},{4,6},{5,3},{6,8},{7,5},{8,10},{9,7},{10,1... | collective-permute-start | bytes 73736 | tf_op jit(solution)/shard_map/ppermute | solution.py:348
  8.3 0.7 %reshape.19.w_ref = bf16[27,32]{1,0:T(8,128)(2,1)S(1)} reshape(bf16[3,3,3,32]{3,2,1,0:T(4,128)(2,1)} %bitcast.15) | data formatting | bytes 3456 | tf_op jit(solution)/shard_map/reshape | solution.py:399
  9.1 0.9 %copy-done.2 = s32[128,384]{1,0:T(8,128)S(1)} copy-done((s32[128,384]{1,0:T(8,128)S(1)}, s32[128,384]{1,0:T(8,128)}, u32[]{:S(2)}) %copy-start.2) | copy-done | bytes 196632
  10.0 0.9 %copy-done.3 = bf16[384,27]{1,0:T(8,128)(2,1)S(1)} copy-done((bf16[384,27]{1,0:T(8,128)(2,1)S(1)}, bf16[384,27]{1,0:T(8,128)(2,1)}, u32[]{:S(2)}) %copy-start.3) | copy-done | bytes 20760
  10.9 0.3 color_weights_kernel.1.w_ref.w1_ref
  11.2 0.0 collective-permute-done.3.next_ref
  11.2 0.0 collective-permute-done.2.near_ref
  11.2 0.0 collective-permute-done.1.far_ref
  11.2 0.0 collective-permute-done.pair_ref
  11.3 3.7 %stats.1 = (bf16[4096,128]{1,0:T(8,128)(2,1)S(1)}, f32[32,128]{1,0:T(8,128)S(1)}) custom-call(bf16[16,12,256]{2,1,0:T(8,128)(2,1)S(1)} %copy.18.own_ref, bf16[16,12,256]{2,1,0:T(8,128)(2,1)S(1)} %collective-permute-done.pair_ref, bf16[16,12,256]{2,1,0:T(8,128)(2,1)S(1)} %collective-permute-done.1.far_ref, ...), custom_call_target="tpu_custom_call" | custom-call | tf_op jit(solution)/shard_map/stats/pallas_call | solution.py:402
  15.0 2.4 %collective-permute-start.4 = (f32[32,128]{1,0:T(8,128)S(1)}, f32[32,128]{1,0:T(8,128)S(1)}, u32[]{:S(2)}, u32[]{:S(2)}) collective-permute-start(f32[32,128]{1,0:T(8,128)S(1)} %get-tuple-element.23), channel_id=1, source_target_pairs={{0,2},{1,3},{2,0},{3,1},{4,6},{5,7},{6,4},{7,5},{8,10},{9,11},{10,... | collective-permute-start | bytes 49160 | tf_op jit(solution)/shard_map/ppermute | solution.py:353
  17.4 0.0 copy-done.5
  17.4 0.0 copy-done.4
  17.4 0.3 feature_weights_kernel.1
  17.7 1.4 %collective-permute-done.4 = f32[32,128]{1,0:T(8,128)S(1)} collective-permute-done((f32[32,128]{1,0:T(8,128)S(1)}, f32[32,128]{1,0:T(8,128)S(1)}, u32[]{:S(2)}, u32[]{:S(2)}) %collective-permute-start.4) | collective-permute-done | bytes 16416 | tf_op jit(solution)/shard_map/ppermute | solution.py:353
  19.1 2.5 %collective-permute-start.5 = (f32[32,128]{1,0:T(8,128)S(1)}, f32[32,128]{1,0:T(8,128)S(1)}, u32[]{:S(2)}, u32[]{:S(2)}) collective-permute-start(f32[32,128]{1,0:T(8,128)S(1)} %pad_maximum_fusion), channel_id=1, source_target_pairs={{0,4},{1,5},{2,6},{3,7},{4,0},{5,1},{6,2},{7,3},{8,12},{9,13},{10,... | collective-permute-start | bytes 49160 | tf_op jit(solution)/shard_map/ppermute | solution.py:353
  21.7 0.0 copy-done.1
  21.7 0.4 hidden_weights_kernel.1.ca_hbm
  22.1 1.3 %collective-permute-done.5 = f32[32,128]{1,0:T(8,128)S(1)} collective-permute-done((f32[32,128]{1,0:T(8,128)S(1)}, f32[32,128]{1,0:T(8,128)S(1)}, u32[]{:S(2)}, u32[]{:S(2)}) %collective-permute-start.5) | collective-permute-done | bytes 16416 | tf_op jit(solution)/shard_map/ppermute | solution.py:353
  23.4 3.1 %collective-permute-start.6 = (f32[32,128]{1,0:T(8,128)S(1)}, f32[32,128]{1,0:T(8,128)S(1)}, u32[]{:S(2)}, u32[]{:S(2)}) collective-permute-start(f32[32,128]{1,0:T(8,128)S(1)} %pad_maximum_fusion.1.st_ref), channel_id=1, source_target_pairs={{0,8},{1,9},{2,10},{3,11},{4,12},{5,13},{6,14},{7,15},{8,0},{9,1},... | collective-permute-start | bytes 49160 | tf_op jit(solution)/shard_map/ppermute | solution.py:353
  26.5 0.0 copy-done
  26.5 0.3 final_weights_kernel.1.cb_hbm
  26.8 1.4 %collective-permute-done.6.other_ref = f32[32,128]{1,0:T(8,128)S(1)} collective-permute-done((f32[32,128]{1,0:T(8,128)S(1)}, f32[32,128]{1,0:T(8,128)S(1)}, u32[]{:S(2)}, u32[]{:S(2)}) %collective-permute-start.6) | collective-permute-done | bytes 16416 | tf_op jit(solution)/shard_map/ppermute | solution.py:353
  28.2 0.0 copy-done.6
  28.2 0.0 copy-done.7
  28.2 0.0 copy-done.8
  28.2 18.9 %main.1 = bf16[12,4,32,256]{3,2,1,0:T(8,128)(2,1)} custom-call(s32[16,12]{1,0:T(8,128)S(1)} %copy-done.6, bf16[4096,128]{1,0:T(8,128)(2,1)S(1)} %get-tuple-element.21.pt_ref, f32[32,128]{1,0:T(8,128)S(1)} %pad_maximum_fusion.1.st_ref, f32[32,128]{1,0:T(8,128)S(1)} %collective-permute-done.6.other_ref, f32[1,32]{1,0:T(1,128)S(1)} %bitcast.12, ...), custom_call_target="tpu_custom_call" | custom-call | tf_op jit(solution)/shard_map/main/pallas_call | solution.py:443
  (14 shorter events, 0.1 us)
Async XLA Ops:
  0.0 17.4 %copy-start.5 = (bf16[3,3,32,32]{3,2,1,0:T(8,128)(2,1)S(1)}, bf16[3,3,32,32]{3,2,1,0:T(8,128)(2,1)}, u32[]{:S(2)}) copy-start(bf16[3,3,32,32]{3,2,1,0:T(8,128)(2,1)} %param.17) | copy-start | bytes 55300
  0.0 17.4 %copy-start.4 = (bf16[3,3,32,32]{3,2,1,0:T(8,128)(2,1)S(1)}, bf16[3,3,32,32]{3,2,1,0:T(8,128)(2,1)}, u32[]{:S(2)}) copy-start(bf16[3,3,32,32]{3,2,1,0:T(8,128)(2,1)} %param.16) | copy-start | bytes 55300
  0.0 21.7 %copy-start.1 = (bf16[3,3,3,32,32]{4,3,2,1,0:T(8,128)(2,1)S(1)}, bf16[3,3,3,32,32]{4,3,2,1,0:T(8,128)(2,1)}, u32[]{:S(2)}) copy-start(bf16[3,3,3,32,32]{4,3,2,1,0:T(8,128)(2,1)} %param.18) | copy-start | bytes 165892
  1.0 25.5 %copy-start = (bf16[3,3,3,32,32]{4,3,2,1,0:T(8,128)(2,1)S(1)}, bf16[3,3,3,32,32]{4,3,2,1,0:T(8,128)(2,1)}, u32[]{:S(2)}) copy-start(bf16[3,3,3,32,32]{4,3,2,1,0:T(8,128)(2,1)} %param.19) | copy-start | bytes 165892
  1.0 10.2 %collective-permute-start.1 = (bf16[16,12,256]{2,1,0:T(8,128)(2,1)S(1)}, bf16[16,12,256]{2,1,0:T(8,128)(2,1)S(1)}, u32[]{:S(2)}, u32[]{:S(2)}) collective-permute-start(bf16[16,12,256]{2,1,0:T(8,128)(2,1)S(1)} %copy.18.own_ref), channel_id=1, source_target_pairs={{0,0},{1,2},{2,1},{3,4},{4,3},{5,6},{6,5},{7,8},{8,7},{9,10},{10,9... | collective-permute-start | bytes 294920 | tf_op jit(solution)/shard_map/ppermute | solution.py:348
  1.8 9.4 %collective-permute-start = (bf16[16,12,256]{2,1,0:T(8,128)(2,1)S(1)}, bf16[16,12,256]{2,1,0:T(8,128)(2,1)S(1)}, u32[]{:S(2)}, u32[]{:S(2)}) collective-permute-start(bf16[16,12,256]{2,1,0:T(8,128)(2,1)S(1)} %copy.18.own_ref), channel_id=1, source_target_pairs={{0,1},{1,0},{2,3},{3,2},{4,5},{5,4},{6,7},{7,6},{8,9},{9,8},{10,11... | collective-permute-start | bytes 294920 | tf_op jit(solution)/shard_map/ppermute | solution.py:353
  6.3 5.0 %collective-permute-start.3 = (bf16[16,3,256]{2,1,0:T(4,128)(2,1)S(1)}, bf16[16,3,256]{2,1,0:T(4,128)(2,1)S(1)}, u32[]{:S(2)}, u32[]{:S(2)}) collective-permute-start(bf16[16,3,256]{2,1,0:T(4,128)(2,1)S(1)} %get-tuple-element.37), channel_id=1, source_target_pairs={{0,1},{1,3},{2,0},{3,5},{4,2},{5,7},{6,4},{7,9},{8,6},{9,11},{10,8... | collective-permute-start | bytes 73736 | tf_op jit(solution)/shard_map/ppermute | solution.py:348
  6.3 4.9 %collective-permute-start.2 = (bf16[16,3,256]{2,1,0:T(4,128)(2,1)S(1)}, bf16[16,3,256]{2,1,0:T(4,128)(2,1)S(1)}, u32[]{:S(2)}, u32[]{:S(2)}) collective-permute-start(bf16[16,3,256]{2,1,0:T(4,128)(2,1)S(1)} %get-tuple-element.38), channel_id=1, source_target_pairs={{0,2},{1,0},{2,4},{3,1},{4,6},{5,3},{6,8},{7,5},{8,10},{9,7},{10,1... | collective-permute-start | bytes 73736 | tf_op jit(solution)/shard_map/ppermute | solution.py:348
  9.1 0.9 %copy-start.2 = (s32[128,384]{1,0:T(8,128)S(1)}, s32[128,384]{1,0:T(8,128)}, u32[]{:S(2)}) copy-start(s32[128,384]{1,0:T(8,128)} %constant.29.clone.tap_ref) | copy-start | bytes 589828
  10.0 0.9 %copy-start.3 = (bf16[384,27]{1,0:T(8,128)(2,1)S(1)}, bf16[384,27]{1,0:T(8,128)(2,1)}, u32[]{:S(2)}) copy-start(bf16[384,27]{1,0:T(8,128)(2,1)} %constant.28.clone.pick_ref) | copy-start | bytes 62212
  15.0 4.1 %collective-permute-start.4 = (f32[32,128]{1,0:T(8,128)S(1)}, f32[32,128]{1,0:T(8,128)S(1)}, u32[]{:S(2)}, u32[]{:S(2)}) collective-permute-start(f32[32,128]{1,0:T(8,128)S(1)} %get-tuple-element.23), channel_id=1, source_target_pairs={{0,2},{1,3},{2,0},{3,1},{4,6},{5,7},{6,4},{7,5},{8,10},{9,11},{10,... | collective-permute-start | bytes 49160 | tf_op jit(solution)/shard_map/ppermute | solution.py:353
  19.1 4.2 %collective-permute-start.5 = (f32[32,128]{1,0:T(8,128)S(1)}, f32[32,128]{1,0:T(8,128)S(1)}, u32[]{:S(2)}, u32[]{:S(2)}) collective-permute-start(f32[32,128]{1,0:T(8,128)S(1)} %pad_maximum_fusion), channel_id=1, source_target_pairs={{0,4},{1,5},{2,6},{3,7},{4,0},{5,1},{6,2},{7,3},{8,12},{9,13},{10,... | collective-permute-start | bytes 49160 | tf_op jit(solution)/shard_map/ppermute | solution.py:353
  21.7 6.6 %copy-start.6 = (s32[16,12]{1,0:T(8,128)S(1)}, s32[16,12]{1,0:T(8,128)}, u32[]{:S(2)}) copy-start(s32[16,12]{1,0:T(8,128)} %shifts.1) | copy-start | bytes 2308
  21.7 6.6 %copy-start.7 = (f32[32]{0:T(128)S(1)}, f32[32]{0:T(128)}, u32[]{:S(2)}) copy-start(f32[32]{0:T(128)} %param.14) | copy-start | bytes 388
  21.7 6.6 %copy-start.8 = (f32[32]{0:T(128)S(1)}, f32[32]{0:T(128)}, u32[]{:S(2)}) copy-start(f32[32]{0:T(128)} %param.15) | copy-start | bytes 388
  23.4 4.8 %collective-permute-start.6 = (f32[32,128]{1,0:T(8,128)S(1)}, f32[32,128]{1,0:T(8,128)S(1)}, u32[]{:S(2)}, u32[]{:S(2)}) collective-permute-start(f32[32,128]{1,0:T(8,128)S(1)} %pad_maximum_fusion.1.st_ref), channel_id=1, source_target_pairs={{0,8},{1,9},{2,10},{3,11},{4,12},{5,13},{6,14},{7,15},{8,0},{9,1},... | collective-permute-start | bytes 49160 | tf_op jit(solution)/shard_map/ppermute | solution.py:353

commit v3 on v2

--- a/solution.py
+++ b/solution.py
@@ -1,7 +1,6 @@
 import functools
 import jax
 import jax.numpy as jnp
-import numpy as np
 from jax import lax
 from jax.experimental import pallas as pl
 from jax.experimental.pallas import tpu as pltpu
@@ -33,6 +32,7 @@
     lane = lax.broadcasted_iota(jnp.int32, (1, width), 1)
     p_scr[...] = jnp.zeros_like(p_scr)
     slots = p_scr.shape[0]
+    apart = views + 1
 
     def some_views(i, carry):
         for slot in range(slots):
@@ -50,7 +50,7 @@
             p_scr[slot, 0:42, :] = jnp.where(lane == 0, 0.0, pltpu.roll(x, 1, 1))
             p_scr[slot, 42:84, :] = x
             p_scr[slot, 84:126, :] = jnp.where(lane == width - 1, 0.0, pltpu.roll(x, width - 1, 1))
-            t_scr[pl.ds(v, width, stride=views), :] = p_scr[slot].T
+            t_scr[pl.ds(v, width, stride=apart), :] = p_scr[slot].T
         return carry
 
     lax.fori_loop(0, views // slots, some_views, 0)
@@ -61,7 +61,8 @@
     total = squares = 0.0
     for i in range(steps):
         rows = slice(i * chunk, (i + 1) * chunk)
-        patch = t_scr[rows, :].astype(BF)
+        columns = range(i * chunk // views, (i + 1) * chunk // views)
+        patch = jnp.concatenate([t_scr[w * apart : w * apart + views, :] for w in columns], axis=0).astype(BF)
         pt_ref[rows, :] = patch
         raw = dot(patch, weight).reshape(chunk // views, views, 256)
         if center is None:
@@ -149,7 +150,7 @@
 
     last_masks = [row_mask(4 * block - 2, 128) for block in range(2)]
     couples = 32
-    apart = 17
+    apart = views + 1
 
     def last(i, carry):
         for block in range(2):
@@ -270,29 +271,21 @@
     return value.astype(BF)
 
 
-def color_weights_kernel(w_ref, pick_ref, tap_ref, w1_ref):
+def color_weights_kernel(w_ref, w1_ref):
     eye = one_hot(32, 384, lambda row, lane: row == (lane & 31)).astype(BF)
     colors = dot(w_ref[...], eye).astype(BF)
-    picked = dot(pick_ref[...], colors)
-    taps = tap_ref[...]
+    place = lax.broadcasted_iota(jnp.int32, (128, 1), 0)
+    tap = (place >= 42).astype(jnp.int32) + (place >= 84).astype(jnp.int32)
+    inner = place - 42 * tap
+    row_in = (inner * 171) >> 9
+    source = jnp.where(place < 126, 3 * tap + inner - 3 * row_in, -99)
+    lane = lax.broadcasted_iota(jnp.int32, (1, 27), 1)
+    row_out = lax.broadcasted_iota(jnp.int32, (1, 384), 1) >> 5
     value = jnp.zeros((128, 384), F32)
     for a in range(3):
-        value = jnp.where(taps == a, picked[a * 128 : a * 128 + 128], value)
+        picked = dot(jnp.where(lane == source + 9 * a, 1.0, 0.0).astype(BF), colors)
+        value = jnp.where(row_out == row_in - a, picked, value)
     w1_ref[...] = value.astype(BF)
-
-
-def color_places(rows_in, rows_out):
-    pick = np.zeros((3, 128, 27), np.float32)
-    taps = np.full((128, rows_out, 32), 3, np.int32)
-    for b in range(3):
-        for row in range(rows_in):
-            for c in range(3):
-                place = (b * rows_in + row) * 3 + c
-                for a in range(3):
-                    pick[a, place, 9 * a + 3 * b + c] = 1.0
-                    if 0 <= row - a < rows_out:
-                        taps[place, row - a] = a
-    return jnp.asarray(pick.reshape(384, 27), BF), jnp.asarray(taps.reshape(128, rows_out * 32))
 
 
 def feature_weights_kernel(wmid_ref, wout_ref, w2_ref, w3_ref):
@@ -397,7 +390,7 @@
     near = send(jnp.where(core == 0, tail, head), "rows", 2, -2)
     after = send(jnp.where(core == 0, head, tail), "rows", -2, 2)
     colors_in = in_weight.transpose(0, 1, 3, 2).reshape(9 * colors, chan)
-    (w1,) = weights(color_weights_kernel, [(128, 384)], colors_in, *color_places(rows + 10, rows + 8))
+    (w1,) = weights(color_weights_kernel, [(128, 384)], colors_in)
 
     patches, stats = pl.pallas_call(
         stats_kernel,
@@ -409,9 +402,9 @@
         in_specs=[VMEM] * 6,
         out_specs=(VMEM, VMEM),
         scratch_shapes=[
-            pltpu.VMEM((4, 48, width), F32),
-            pltpu.VMEM((4, 128, width), F32),
-            pltpu.VMEM((total, 128), F32),
+            pltpu.VMEM((8, 48, width), F32),
+            pltpu.VMEM((8, 128, width), F32),
+            pltpu.VMEM(((width + 1) * (views + 1), 128), F32),
         ],
         compiler_params=limit(12),
     )(own, pair, far, near, after, w1)
@@ -427,7 +420,8 @@
         other = swap(stats, "rows", bit)
         while jobs:
             kernel, shapes, operands = jobs.pop(0)
-            stats, operands = lax.optimization_barrier((stats, operands))
+            if bit > 2:
+                stats, operands = lax.optimization_barrier((stats, operands))
             new = weights(kernel, shapes, *operands)
             if not last:
                 other, new = lax.optimization_barrier((other, new))
@@ -449,7 +443,7 @@
         scratch_shapes=[
             pltpu.VMEM((total + 2 * views, 384), BF),
             pltpu.VMEM((2, total + 2 * views, 256), BF),
-            pltpu.VMEM((2 * width * 17, 128), F32),
+            pltpu.VMEM(((2 * width + 1) * (views + 1), 128), F32),
             *[pltpu.VMEM((9, width + 2 * REACH, 128), F32) for _ in range(4)],
             pltpu.VMEM((8, width + 16, 256), F32),
             pltpu.VMEM((planes + 2, width, 768), BF),

time: 47.5 us -> 46.9 us (0.987)
  starting transfers between devices: 15.3 us -> 15.9 us
  Pallas kernels: 23.9 us -> 23.3 us
  waiting for transfers between devices: 4.12 us -> 3.57 us
    ppermute x4, waiting for transfers between devices: 4.11 us -> 2.7 us  [swap(): return lax.ppermute(value, axis, [(i, i ^ bit) for i in range(count)])]
    ppermute x3, waiting for transfers between devices: 0.01 us -> 0.87 us  [send(): return lax.ppermute(value, axis, pairs)]
    ppermute x4, starting transfers between devices: 12.4 us -> 13.2 us  [swap(): return lax.ppermute(value, axis, [(i, i ^ bit) for i in range(count)])]
    pallas_call x1, Pallas kernels: 3.71 us -> 3.06 us  [shards(): pl.pallas_call(stats_kernel, name='stats', out_shape=(jax.ShapeDtypeStruc...]
    unnamed x19 -> x15, local copies, waits for them, and re-layouts: 2.79 us -> 2.74 us
where the time goes in v3:
time: 46.9 us; the launch traced here: 46.7 us
  Pallas kernels  23.3 us (50%)
  starting transfers between devices  15.9 us (34%)
  waiting for transfers between devices  3.57 us (8%)
  local copies, waits for them, and re-layouts  3.49 us (7%)
    pallas_call x1, Pallas kernels, shards(): pl.pallas_call(main_kernel, name='main', out_shape=jax.ShapeDtypeStruct((...  18.9 us
    ppermute x4, starting transfers between devices, swap(): return lax.ppermute(value, axis, [(i, i ^ bit) for i in range(count)])  13.2 us
    pallas_call x1, Pallas kernels, shards(): pl.pallas_call(stats_kernel, name='stats', out_shape=(jax.ShapeDtypeStruc...  3.06 us
    ppermute x3, starting transfers between devices, send(): return lax.ppermute(value, axis, pairs)  2.75 us
    unnamed x15, local copies, waits for them, and re-layouts  2.74 us
    ppermute x4, waiting for transfers between devices, swap(): return lax.ppermute(value, axis, [(i, i ^ bit) for i in range(count)])  2.7 us
    pallas_call x4, Pallas kernels, weights(): pl.pallas_call(kernel, name=kernel.__name__, out_shape=shapes, in_specs=[...  1.35 us
  transfers between devices with their start and end apart: 7, of which 3 were waited for; matrix products, arithmetic and copies ran while one was open for 2% of the time, Pallas kernels for 3%

profile of v3, /device:TPU:0, one launch (start us, length us, event | category | flops | bytes accessed | tf_op | source)
XLA Modules:
  0.0 46.7 jit_solution(6708023136063075287)
XLA Ops:
  0.0 0.0 copy-start.1
  0.0 0.0 copy-start
  0.0 1.0 %copy.11 = bf16[16,4,3,256]{3,0,2,1:T(8,128)(2,1)S(1)} copy(bf16[16,4,3,256]{3,1,2,0:T(4,128)(2,1)} %param.9) | data formatting | bytes 196608 | tf_op args[0]
  1.0 0.7 %collective-permute-start.1 = (bf16[16,12,256]{2,1,0:T(8,128)(2,1)S(1)}, bf16[16,12,256]{2,1,0:T(8,128)(2,1)S(1)}, u32[]{:S(2)}, u32[]{:S(2)}) collective-permute-start(bf16[16,12,256]{2,1,0:T(8,128)(2,1)S(1)} %copy.16.own_ref), channel_id=1, source_target_pairs={{0,0},{1,2},{2,1},{3,4},{4,3},{5,6},{6,5},{7,8},{8,7},{9,10},{10,9... | collective-permute-start | bytes 294920 | tf_op jit(solution)/shard_map/ppermute | solution.py:341
  1.7 4.4 %collective-permute-start = (bf16[16,12,256]{2,1,0:T(8,128)(2,1)S(1)}, bf16[16,12,256]{2,1,0:T(8,128)(2,1)S(1)}, u32[]{:S(2)}, u32[]{:S(2)}) collective-permute-start(bf16[16,12,256]{2,1,0:T(8,128)(2,1)S(1)} %copy.16.own_ref), channel_id=1, source_target_pairs={{0,1},{1,0},{2,3},{3,2},{4,5},{5,4},{6,7},{7,6},{8,9},{9,8},{10,11... | collective-permute-start | bytes 294920 | tf_op jit(solution)/shard_map/ppermute | solution.py:346
  6.1 0.1 collective-permute-start.3
  6.2 2.0 %collective-permute-start.2 = (bf16[16,3,256]{2,1,0:T(4,128)(2,1)S(1)}, bf16[16,3,256]{2,1,0:T(4,128)(2,1)S(1)}, u32[]{:S(2)}, u32[]{:S(2)}) collective-permute-start(bf16[16,3,256]{2,1,0:T(4,128)(2,1)S(1)} %get-tuple-element.32), channel_id=1, source_target_pairs={{0,2},{1,0},{2,4},{3,1},{4,6},{5,3},{6,8},{7,5},{8,10},{9,7},{10,1... | collective-permute-start | bytes 73736 | tf_op jit(solution)/shard_map/ppermute | solution.py:341
  8.2 0.7 %reshape.19.w_ref = bf16[27,32]{1,0:T(8,128)(2,1)S(1)} reshape(bf16[3,3,3,32]{3,2,1,0:T(4,128)(2,1)} %bitcast.15) | data formatting | bytes 3456 | tf_op jit(solution)/shard_map/reshape | solution.py:392
  8.9 0.3 color_weights_kernel.1.w_ref.w1_ref
  9.3 0.9 %collective-permute-done.3.next_ref = bf16[16,3,256]{2,1,0:T(4,128)(2,1)S(1)} collective-permute-done((bf16[16,3,256]{2,1,0:T(4,128)(2,1)S(1)}, bf16[16,3,256]{2,1,0:T(4,128)(2,1)S(1)}, u32[]{:S(2)}, u32[]{:S(2)}) %collective-permute-start.3) | collective-permute-done | bytes 24608 | tf_op jit(solution)/shard_map/ppermute | solution.py:341
  10.1 0.0 collective-permute-done.2.near_ref
  10.1 0.0 collective-permute-done.1.far_ref
  10.1 0.0 collective-permute-done.pair_ref
  10.1 3.1 %stats.1 = (bf16[4096,128]{1,0:T(8,128)(2,1)S(1)}, f32[32,128]{1,0:T(8,128)S(1)}) custom-call(bf16[16,12,256]{2,1,0:T(8,128)(2,1)S(1)} %copy.16.own_ref, bf16[16,12,256]{2,1,0:T(8,128)(2,1)S(1)} %collective-permute-done.pair_ref, bf16[16,12,256]{2,1,0:T(8,128)(2,1)S(1)} %collective-permute-done.1.far_ref, ...), custom_call_target="tpu_custom_call" | custom-call | tf_op jit(solution)/shard_map/stats/pallas_call | solution.py:395
  13.2 2.9 %collective-permute-start.4 = (f32[32,128]{1,0:T(8,128)S(1)}, f32[32,128]{1,0:T(8,128)S(1)}, u32[]{:S(2)}, u32[]{:S(2)}) collective-permute-start(f32[32,128]{1,0:T(8,128)S(1)} %get-tuple-element.19), channel_id=1, source_target_pairs={{0,2},{1,3},{2,0},{3,1},{4,6},{5,7},{6,4},{7,5},{8,10},{9,11},{10,... | collective-permute-start | bytes 49160 | tf_op jit(solution)/shard_map/ppermute | solution.py:346
  16.1 0.0 copy-start.2
  16.1 0.9 %copy-done.2 = bf16[3,3,32,32]{3,2,1,0:T(8,128)(2,1)S(1)} copy-done((bf16[3,3,32,32]{3,2,1,0:T(8,128)(2,1)S(1)}, bf16[3,3,32,32]{3,2,1,0:T(8,128)(2,1)}, u32[]{:S(2)}) %copy-start.2) | copy-done | bytes 18456
  17.0 0.9 %copy-done.3 = bf16[3,3,32,32]{3,2,1,0:T(8,128)(2,1)S(1)} copy-done((bf16[3,3,32,32]{3,2,1,0:T(8,128)(2,1)S(1)}, bf16[3,3,32,32]{3,2,1,0:T(8,128)(2,1)}, u32[]{:S(2)}) %copy-start.3) | copy-done | bytes 18456
  17.9 0.3 feature_weights_kernel.1
  18.2 0.0 collective-permute-done.4
  18.2 2.6 %collective-permute-start.5 = (f32[32,128]{1,0:T(8,128)S(1)}, f32[32,128]{1,0:T(8,128)S(1)}, u32[]{:S(2)}, u32[]{:S(2)}) collective-permute-start(f32[32,128]{1,0:T(8,128)S(1)} %pad_maximum_fusion), channel_id=1, source_target_pairs={{0,4},{1,5},{2,6},{3,7},{4,0},{5,1},{6,2},{7,3},{8,12},{9,13},{10,... | collective-permute-start | bytes 49160 | tf_op jit(solution)/shard_map/ppermute | solution.py:346
  20.9 0.0 copy-done.1
  20.9 0.4 hidden_weights_kernel.1.ca_hbm
  21.3 1.3 %collective-permute-done.5 = f32[32,128]{1,0:T(8,128)S(1)} collective-permute-done((f32[32,128]{1,0:T(8,128)S(1)}, f32[32,128]{1,0:T(8,128)S(1)}, u32[]{:S(2)}, u32[]{:S(2)}) %collective-permute-start.5) | collective-permute-done | bytes 16416 | tf_op jit(solution)/shard_map/ppermute | solution.py:346
  22.6 3.2 %collective-permute-start.6 = (f32[32,128]{1,0:T(8,128)S(1)}, f32[32,128]{1,0:T(8,128)S(1)}, u32[]{:S(2)}, u32[]{:S(2)}) collective-permute-start(f32[32,128]{1,0:T(8,128)S(1)} %pad_maximum_fusion.1.st_ref), channel_id=1, source_target_pairs={{0,8},{1,9},{2,10},{3,11},{4,12},{5,13},{6,14},{7,15},{8,0},{9,1},... | collective-permute-start | bytes 49160 | tf_op jit(solution)/shard_map/ppermute | solution.py:346
  25.8 0.0 copy-done
  25.8 0.3 final_weights_kernel.1.cb_hbm
  26.1 1.4 %collective-permute-done.6.other_ref = f32[32,128]{1,0:T(8,128)S(1)} collective-permute-done((f32[32,128]{1,0:T(8,128)S(1)}, f32[32,128]{1,0:T(8,128)S(1)}, u32[]{:S(2)}, u32[]{:S(2)}) %collective-permute-start.6) | collective-permute-done | bytes 16416 | tf_op jit(solution)/shard_map/ppermute | solution.py:346
  27.5 0.0 copy-done.4
  27.5 0.0 copy-done.5
  27.5 0.0 copy-done.6
  27.5 18.9 %main.1 = bf16[12,4,32,256]{3,2,1,0:T(8,128)(2,1)} custom-call(s32[16,12]{1,0:T(8,128)S(1)} %copy-done.4, bf16[4096,128]{1,0:T(8,128)(2,1)S(1)} %get-tuple-element.18.pt_ref, f32[32,128]{1,0:T(8,128)S(1)} %pad_maximum_fusion.1.st_ref, f32[32,128]{1,0:T(8,128)S(1)} %collective-permute-done.6.other_ref, f32[1,32]{1,0:T(1,128)S(1)} %bitcast.12, ...), custom_call_target="tpu_custom_call" | custom-call | tf_op jit(solution)/shard_map/main/pallas_call | solution.py:437
  (10 shorter events, 0.1 us)
Async XLA Ops:
  0.0 20.9 %copy-start.1 = (bf16[3,3,3,32,32]{4,3,2,1,0:T(8,128)(2,1)S(1)}, bf16[3,3,3,32,32]{4,3,2,1,0:T(8,128)(2,1)}, u32[]{:S(2)}) copy-start(bf16[3,3,3,32,32]{4,3,2,1,0:T(8,128)(2,1)} %param.16) | copy-start | bytes 165892
  0.0 25.8 %copy-start = (bf16[3,3,3,32,32]{4,3,2,1,0:T(8,128)(2,1)S(1)}, bf16[3,3,3,32,32]{4,3,2,1,0:T(8,128)(2,1)}, u32[]{:S(2)}) copy-start(bf16[3,3,3,32,32]{4,3,2,1,0:T(8,128)(2,1)} %param.17) | copy-start | bytes 165892
  1.0 9.1 %collective-permute-start.1 = (bf16[16,12,256]{2,1,0:T(8,128)(2,1)S(1)}, bf16[16,12,256]{2,1,0:T(8,128)(2,1)S(1)}, u32[]{:S(2)}, u32[]{:S(2)}) collective-permute-start(bf16[16,12,256]{2,1,0:T(8,128)(2,1)S(1)} %copy.16.own_ref), channel_id=1, source_target_pairs={{0,0},{1,2},{2,1},{3,4},{4,3},{5,6},{6,5},{7,8},{8,7},{9,10},{10,9... | collective-permute-start | bytes 294920 | tf_op jit(solution)/shard_map/ppermute | solution.py:341
  1.7 8.5 %collective-permute-start = (bf16[16,12,256]{2,1,0:T(8,128)(2,1)S(1)}, bf16[16,12,256]{2,1,0:T(8,128)(2,1)S(1)}, u32[]{:S(2)}, u32[]{:S(2)}) collective-permute-start(bf16[16,12,256]{2,1,0:T(8,128)(2,1)S(1)} %copy.16.own_ref), channel_id=1, source_target_pairs={{0,1},{1,0},{2,3},{3,2},{4,5},{5,4},{6,7},{7,6},{8,9},{9,8},{10,11... | collective-permute-start | bytes 294920 | tf_op jit(solution)/shard_map/ppermute | solution.py:346
  6.1 4.0 %collective-permute-start.3 = (bf16[16,3,256]{2,1,0:T(4,128)(2,1)S(1)}, bf16[16,3,256]{2,1,0:T(4,128)(2,1)S(1)}, u32[]{:S(2)}, u32[]{:S(2)}) collective-permute-start(bf16[16,3,256]{2,1,0:T(4,128)(2,1)S(1)} %get-tuple-element.31), channel_id=1, source_target_pairs={{0,1},{1,3},{2,0},{3,5},{4,2},{5,7},{6,4},{7,9},{8,6},{9,11},{10,8... | collective-permute-start | bytes 73736 | tf_op jit(solution)/shard_map/ppermute | solution.py:341
  6.2 3.9 %collective-permute-start.2 = (bf16[16,3,256]{2,1,0:T(4,128)(2,1)S(1)}, bf16[16,3,256]{2,1,0:T(4,128)(2,1)S(1)}, u32[]{:S(2)}, u32[]{:S(2)}) collective-permute-start(bf16[16,3,256]{2,1,0:T(4,128)(2,1)S(1)} %get-tuple-element.32), channel_id=1, source_target_pairs={{0,2},{1,0},{2,4},{3,1},{4,6},{5,3},{6,8},{7,5},{8,10},{9,7},{10,1... | collective-permute-start | bytes 73736 | tf_op jit(solution)/shard_map/ppermute | solution.py:341
  13.2 5.0 %collective-permute-start.4 = (f32[32,128]{1,0:T(8,128)S(1)}, f32[32,128]{1,0:T(8,128)S(1)}, u32[]{:S(2)}, u32[]{:S(2)}) collective-permute-start(f32[32,128]{1,0:T(8,128)S(1)} %get-tuple-element.19), channel_id=1, source_target_pairs={{0,2},{1,3},{2,0},{3,1},{4,6},{5,7},{6,4},{7,5},{8,10},{9,11},{10,... | collective-permute-start | bytes 49160 | tf_op jit(solution)/shard_map/ppermute | solution.py:346
  16.1 0.9 %copy-start.2 = (bf16[3,3,32,32]{3,2,1,0:T(8,128)(2,1)S(1)}, bf16[3,3,32,32]{3,2,1,0:T(8,128)(2,1)}, u32[]{:S(2)}) copy-start(bf16[3,3,32,32]{3,2,1,0:T(8,128)(2,1)} %param.14) | copy-start | bytes 55300
  17.0 0.9 %copy-start.3 = (bf16[3,3,32,32]{3,2,1,0:T(8,128)(2,1)S(1)}, bf16[3,3,32,32]{3,2,1,0:T(8,128)(2,1)}, u32[]{:S(2)}) copy-start(bf16[3,3,32,32]{3,2,1,0:T(8,128)(2,1)} %param.15) | copy-start | bytes 55300
  18.2 4.3 %collective-permute-start.5 = (f32[32,128]{1,0:T(8,128)S(1)}, f32[32,128]{1,0:T(8,128)S(1)}, u32[]{:S(2)}, u32[]{:S(2)}) collective-permute-start(f32[32,128]{1,0:T(8,128)S(1)} %pad_maximum_fusion), channel_id=1, source_target_pairs={{0,4},{1,5},{2,6},{3,7},{4,0},{5,1},{6,2},{7,3},{8,12},{9,13},{10,... | collective-permute-start | bytes 49160 | tf_op jit(solution)/shard_map/ppermute | solution.py:346
  20.9 6.7 %copy-start.4 = (s32[16,12]{1,0:T(8,128)S(1)}, s32[16,12]{1,0:T(8,128)}, u32[]{:S(2)}) copy-start(s32[16,12]{1,0:T(8,128)} %shifts.1) | copy-start | bytes 2308
  20.9 6.7 %copy-start.5 = (f32[32]{0:T(128)S(1)}, f32[32]{0:T(128)}, u32[]{:S(2)}) copy-start(f32[32]{0:T(128)} %param.12) | copy-start | bytes 388
  20.9 6.7 %copy-start.6 = (f32[32]{0:T(128)S(1)}, f32[32]{0:T(128)}, u32[]{:S(2)}) copy-start(f32[32]{0:T(128)} %param.13) | copy-start | bytes 388
  22.6 4.9 %collective-permute-start.6 = (f32[32,128]{1,0:T(8,128)S(1)}, f32[32,128]{1,0:T(8,128)S(1)}, u32[]{:S(2)}, u32[]{:S(2)}) collective-permute-start(f32[32,128]{1,0:T(8,128)S(1)} %pad_maximum_fusion.1.st_ref), channel_id=1, source_target_pairs={{0,8},{1,9},{2,10},{3,11},{4,12},{5,13},{6,14},{7,15},{8,0},{9,1},... | collective-permute-start | bytes 49160 | tf_op jit(solution)/shard_map/ppermute | solution.py:346

commit v4 on v3

--- a/solution.py
+++ b/solution.py
@@ -77,6 +77,12 @@
     st_ref[views:, :] = fold(squares) - offset * offset * (8.0 * width)
 
 
+def raw_kernel(start, pt_ref, w1_ref, raw_ref):
+    for i in range(raw_ref.shape[0] // 1024):
+        rows = slice(i * 1024, (i + 1) * 1024)
+        raw_ref[rows, :] = dot(pt_ref[start + i * 1024 : start + (i + 1) * 1024, :], w1_ref[...])
+
+
 def row_mask(first, lanes):
     row = lax.axis_index("rows") * 4 + first + (lax.broadcasted_iota(jnp.int32, (1, lanes), 1) >> 5)
     return jnp.where((row >= 0) & (row < lax.axis_size("rows") * 4), 1.0, 0.0).astype(F32)
@@ -95,7 +101,7 @@
 
 
 def main_kernel(
-    shifts, pt_ref, st_ref, other_ref, gain_ref, bias_ref, w1_ref, w2_ref, w3_ref, ca_hbm, cb_hbm, out_ref,
+    shifts, low_ref, high_ref, st_ref, other_ref, gain_ref, bias_ref, w2_ref, w3_ref, ca_hbm, cb_hbm, out_ref,
     nb, mid, f_scr, s_low, s_high, q_low, q_high, v32, vb, hb, ca_ref, cb_ref, g_scr, sems,
 ):
     copies = [
@@ -106,7 +112,7 @@
         copy.start()
     s_scr, q_scr = (s_low, s_high), (q_low, q_high)
     views = st_ref.shape[0] // 2
-    total = pt_ref.shape[0]
+    total = 2 * low_ref.shape[0]
     planes = out_ref.shape[0]
     width = out_ref.shape[3]
     cells = lax.axis_size("rows") * 4 * width
@@ -125,9 +131,10 @@
     masks = [row_mask(4 * group - 4, 128) for group in range(3)]
 
     def normalize(i, carry):
-        rows = pl.ds(pl.multiple_of(i * size, size), size)
         out = pl.ds(pl.multiple_of(i * size + views, views), size)
-        raw = dot(pt_ref[rows, :], w1_ref[...])
+        half = steps // 2
+        raw_ref = low_ref if i < half else high_ref
+        raw = raw_ref[i % half * size : (i % half + 1) * size, :]
         for group in range(3):
             part = raw[:, group * 128 : group * 128 + 128].reshape(cols, views, 128)
             part = jnp.maximum((part - mean[None]) * scale[None] + shift[None], 0.0) * masks[group][None]
@@ -413,11 +420,26 @@
         (hidden_weights_kernel, [(3, 768, 256)], (cost_weight_a.reshape(27, chan, chan),)),
         (final_weights_kernel, [(4, 768, 256)], (cost_weight_b.reshape(27, chan, chan),)),
     ]
-    made = []
+    made, raw = [], []
     bit = 2
     while True:
         last = 2 * bit >= count
         other = swap(stats, "rows", bit)
+        last = 2 * bit >= count
+        if last or 4 * bit >= count:
+            stats, source = lax.optimization_barrier((stats, patches))
+            half = pl.pallas_call(
+                functools.partial(raw_kernel, len(raw) * (total // 2)),
+                name="raw",
+                out_shape=jax.ShapeDtypeStruct((total // 2, 384), F32),
+                in_specs=[VMEM] * 2,
+                out_specs=VMEM,
+                cost_estimate=pl.CostEstimate(flops=total * 128 * 384, bytes_accessed=4000000, transcendentals=0),
+                compiler_params=limit(8),
+            )(source, w1)
+            if not last:
+                other, half = lax.optimization_barrier((other, half))
+            raw.append(half)
         while jobs:
             kernel, shapes, operands = jobs.pop(0)
             if bit > 2:
@@ -453,8 +475,8 @@
             pltpu.VMEM((8, 128), F32),
             pltpu.SemaphoreType.DMA((2,)),
         ],
-        compiler_params=limit(44),
-    )(shifts, patches, stats, other, norm_gain[None], norm_bias[None], w1, w2, w3, ca, cb)
+        compiler_params=limit(40),
+    )(shifts, *raw, stats, other, norm_gain[None], norm_bias[None], w2, w3, ca, cb)
 
 
 def solution(mesh):

time: 46.9 us -> 45.8 us (0.977)
  starting transfers between devices: 15.9 us -> 12.6 us
  waiting for transfers between devices: 3.57 us -> 4.92 us
  local copies, waits for them, and re-layouts: 3.49 us -> 4.38 us
    ppermute x4, starting transfers between devices: 13.2 us -> 7.93 us  [swap(): return lax.ppermute(value, axis, [(i, i ^ bit) for i in range(count)])]
    ppermute x3, waiting for transfers between devices: 0.87 us -> 3.65 us  [send(): return lax.ppermute(value, axis, pairs)]
    ppermute x3, starting transfers between devices: 2.75 us -> 4.68 us  [send(): return lax.ppermute(value, axis, pairs)]
    ppermute x4, waiting for transfers between devices: 2.7 us -> 1.26 us  [swap(): return lax.ppermute(value, axis, [(i, i ^ bit) for i in range(count)])]
    pallas_call x1, Pallas kernels: 18.9 us -> 17.8 us  [shards(): pl.pallas_call(main_kernel, name='main', out_shape=jax.ShapeDtypeStruct((...]
    pallas_call x0 -> x2, Pallas kernels: none -> 1.1 us  [shards(): pl.pallas_call(functools.partial(raw_kernel, len(raw) * (total // 2)), na...]
    unnamed x15, local copies, waits for them, and re-layouts: 2.74 us -> 3.63 us
  transfers between devices with their start and end apart: 7 -> 7, of which waited for: 3 -> 4; matrix products, arithmetic and copies ran while one was open for 2% -> 2% of each run, Pallas kernels for 3% -> 5%
where the time goes in v4:
time: 45.8 us; the launch traced here: 45.5 us
  Pallas kernels  23.3 us (51%)
  starting transfers between devices  12.6 us (28%)
  waiting for transfers between devices  4.92 us (11%)
  local copies, waits for them, and re-layouts  4.38 us (10%)
    pallas_call x1, Pallas kernels, shards(): pl.pallas_call(main_kernel, name='main', out_shape=jax.ShapeDtypeStruct((...  17.8 us
    ppermute x4, starting transfers between devices, swap(): return lax.ppermute(value, axis, [(i, i ^ bit) for i in range(count)])  7.93 us
    ppermute x3, starting transfers between devices, send(): return lax.ppermute(value, axis, pairs)  4.68 us
    ppermute x3, waiting for transfers between devices, send(): return lax.ppermute(value, axis, pairs)  3.65 us
    unnamed x15, local copies, waits for them, and re-layouts  3.63 us
    pallas_call x1, Pallas kernels, shards(): pl.pallas_call(stats_kernel, name='stats', out_shape=(jax.ShapeDtypeStruc...  3.06 us
    pallas_call x4, Pallas kernels, weights(): pl.pallas_call(kernel, name=kernel.__name__, out_shape=shapes, in_specs=[...  1.35 us
    ppermute x4, waiting for transfers between devices, swap(): return lax.ppermute(value, axis, [(i, i ^ bit) for i in range(count)])  1.26 us
  transfers between devices with their start and end apart: 7, of which 4 were waited for; matrix products, arithmetic and copies ran while one was open for 2% of the time, Pallas kernels for 5%

profile of v4, /device:TPU:0, one launch (start us, length us, event | category | flops | bytes accessed | tf_op | source)
XLA Modules:
  0.0 45.5 jit_solution(7754033146124676702)
XLA Ops:
  0.0 0.9 %copy.11 = bf16[16,4,3,256]{3,0,2,1:T(8,128)(2,1)S(1)} copy(bf16[16,4,3,256]{3,1,2,0:T(4,128)(2,1)} %param.9) | data formatting | bytes 196608 | tf_op args[0]
  0.9 0.5 %collective-permute-start = (bf16[16,12,256]{2,1,0:T(8,128)(2,1)S(1)}, bf16[16,12,256]{2,1,0:T(8,128)(2,1)S(1)}, u32[]{:S(2)}, u32[]{:S(2)}) collective-permute-start(bf16[16,12,256]{2,1,0:T(8,128)(2,1)S(1)} %copy.16.own_ref), channel_id=1, source_target_pairs={{0,1},{1,0},{2,3},{3,2},{4,5},{5,4},{6,7},{7,6},{8,9},{9,8},{10,11... | collective-permute-start | bytes 294920 | tf_op jit(solution)/shard_map/ppermute | solution.py:353
  1.5 0.7 %collective-permute-start.1 = (bf16[16,12,256]{2,1,0:T(8,128)(2,1)S(1)}, bf16[16,12,256]{2,1,0:T(8,128)(2,1)S(1)}, u32[]{:S(2)}, u32[]{:S(2)}) collective-permute-start(bf16[16,12,256]{2,1,0:T(8,128)(2,1)S(1)} %copy.16.own_ref), channel_id=1, source_target_pairs={{0,0},{1,2},{2,1},{3,4},{4,3},{5,6},{6,5},{7,8},{8,7},{9,10},{10,9... | collective-permute-start | bytes 294920 | tf_op jit(solution)/shard_map/ppermute | solution.py:348
  2.2 3.8 %collective-permute-start.2 = (bf16[16,3,256]{2,1,0:T(4,128)(2,1)S(1)}, bf16[16,3,256]{2,1,0:T(4,128)(2,1)S(1)}, u32[]{:S(2)}, u32[]{:S(2)}) collective-permute-start(bf16[16,3,256]{2,1,0:T(4,128)(2,1)S(1)} %get-tuple-element.44), channel_id=1, source_target_pairs={{0,2},{1,0},{2,4},{3,1},{4,6},{5,3},{6,8},{7,5},{8,10},{9,7},{10,1... | collective-permute-start | bytes 73736 | tf_op jit(solution)/shard_map/ppermute | solution.py:348
  6.0 0.2 collective-permute-start.3
  6.2 0.7 %reshape.19.w_ref = bf16[27,32]{1,0:T(8,128)(2,1)S(1)} reshape(bf16[3,3,3,32]{3,2,1,0:T(4,128)(2,1)} %bitcast.15) | data formatting | bytes 3456 | tf_op jit(solution)/shard_map/reshape | solution.py:399
  6.9 0.3 color_weights_kernel.1.w_ref.w1_ref
  7.3 0.5 %collective-permute-done.2.near_ref = bf16[16,3,256]{2,1,0:T(4,128)(2,1)S(1)} collective-permute-done((bf16[16,3,256]{2,1,0:T(4,128)(2,1)S(1)}, bf16[16,3,256]{2,1,0:T(4,128)(2,1)S(1)}, u32[]{:S(2)}, u32[]{:S(2)}) %collective-permute-start.2) | collective-permute-done | bytes 24608 | tf_op jit(solution)/shard_map/ppermute | solution.py:348
  7.8 3.1 %collective-permute-done.3.next_ref = bf16[16,3,256]{2,1,0:T(4,128)(2,1)S(1)} collective-permute-done((bf16[16,3,256]{2,1,0:T(4,128)(2,1)S(1)}, bf16[16,3,256]{2,1,0:T(4,128)(2,1)S(1)}, u32[]{:S(2)}, u32[]{:S(2)}) %collective-permute-start.3) | collective-permute-done | bytes 24608 | tf_op jit(solution)/shard_map/ppermute | solution.py:348
  10.9 0.0 collective-permute-done.pair_ref
  10.9 0.0 collective-permute-done.1.far_ref
  10.9 3.1 %stats.1 = (bf16[4096,128]{1,0:T(8,128)(2,1)S(1)}, f32[32,128]{1,0:T(8,128)S(1)}) custom-call(bf16[16,12,256]{2,1,0:T(8,128)(2,1)S(1)} %copy.16.own_ref, bf16[16,12,256]{2,1,0:T(8,128)(2,1)S(1)} %collective-permute-done.pair_ref, bf16[16,12,256]{2,1,0:T(8,128)(2,1)S(1)} %collective-permute-done.1.far_ref, ...), custom_call_target="tpu_custom_call" | custom-call | tf_op jit(solution)/shard_map/stats/pallas_call | solution.py:402
  14.0 3.0 %collective-permute-start.4 = (f32[32,128]{1,0:T(8,128)S(1)}, f32[32,128]{1,0:T(8,128)S(1)}, u32[]{:S(2)}, u32[]{:S(2)}) collective-permute-start(f32[32,128]{1,0:T(8,128)S(1)} %get-tuple-element.24), channel_id=1, source_target_pairs={{0,2},{1,3},{2,0},{3,1},{4,6},{5,7},{6,4},{7,5},{8,10},{9,11},{10,... | collective-permute-start | bytes 49160 | tf_op jit(solution)/shard_map/ppermute | solution.py:353
  17.0 0.9 %copy-done.2 = bf16[3,3,32,32]{3,2,1,0:T(8,128)(2,1)S(1)} copy-done((bf16[3,3,32,32]{3,2,1,0:T(8,128)(2,1)S(1)}, bf16[3,3,32,32]{3,2,1,0:T(8,128)(2,1)}, u32[]{:S(2)}) %copy-start.2) | copy-done | bytes 18456
  17.9 0.9 %copy-done.3 = bf16[3,3,32,32]{3,2,1,0:T(8,128)(2,1)S(1)} copy-done((bf16[3,3,32,32]{3,2,1,0:T(8,128)(2,1)S(1)}, bf16[3,3,32,32]{3,2,1,0:T(8,128)(2,1)}, u32[]{:S(2)}) %copy-start.3) | copy-done | bytes 18456
  18.7 0.3 feature_weights_kernel.1
  19.0 0.0 collective-permute-done.4
  19.1 1.7 %collective-permute-start.5 = (f32[32,128]{1,0:T(8,128)S(1)}, f32[32,128]{1,0:T(8,128)S(1)}, u32[]{:S(2)}, u32[]{:S(2)}) collective-permute-start(f32[32,128]{1,0:T(8,128)S(1)} %pad_maximum_fusion), channel_id=1, source_target_pairs={{0,4},{1,5},{2,6},{3,7},{4,0},{5,1},{6,2},{7,3},{8,12},{9,13},{10,... | collective-permute-start | bytes 49160 | tf_op jit(solution)/shard_map/ppermute | solution.py:353
  20.8 0.9 %copy-done.1 = bf16[3,3,3,32,32]{4,3,2,1,0:T(8,128)(2,1)S(1)} copy-done((bf16[3,3,3,32,32]{4,3,2,1,0:T(8,128)(2,1)S(1)}, bf16[3,3,3,32,32]{4,3,2,1,0:T(8,128)(2,1)}, u32[]{:S(2)}) %copy-start.1) | copy-done | bytes 55320
  21.7 0.4 hidden_weights_kernel.1.ca_hbm
  22.1 0.6 %raw.2.low_ref = f32[2048,384]{1,0:T(8,128)S(1)} custom-call(bf16[4096,128]{1,0:T(8,128)(2,1)S(1)} %get-tuple-element.36.pt_ref, bf16[128,384]{1,0:T(8,128)(2,1)S(1)} %color_weights_kernel.1.w_ref.w1_ref), custom_call_target="tpu_custom_call" | custom-call | flops 201326592 | bytes 4000000 | tf_op jit(solution)/shard_map/raw/pallas_call | solution.py:431
  22.7 0.0 copy-start.4
  22.7 0.0 copy-start.5
  22.7 0.0 copy-start.6
  22.7 0.2 collective-permute-done.5
  22.9 2.8 %collective-permute-start.6 = (f32[32,128]{1,0:T(8,128)S(1)}, f32[32,128]{1,0:T(8,128)S(1)}, u32[]{:S(2)}, u32[]{:S(2)}) collective-permute-start(f32[32,128]{1,0:T(8,128)S(1)} %pad_maximum_fusion.1.st_ref), channel_id=1, source_target_pairs={{0,8},{1,9},{2,10},{3,11},{4,12},{5,13},{6,14},{7,15},{8,0},{9,1},... | collective-permute-start | bytes 49160 | tf_op jit(solution)/shard_map/ppermute | solution.py:353
  25.7 0.0 copy-done
  25.7 0.3 final_weights_kernel.1.cb_hbm
  26.0 0.5 %raw.3.high_ref = f32[2048,384]{1,0:T(8,128)S(1)} custom-call(bf16[4096,128]{1,0:T(8,128)(2,1)S(1)} %get-tuple-element.36.pt_ref, bf16[128,384]{1,0:T(8,128)(2,1)S(1)} %color_weights_kernel.1.w_ref.w1_ref), custom_call_target="tpu_custom_call" | custom-call | flops 201326592 | bytes 4000000 | tf_op jit(solution)/shard_map/raw/pallas_call | solution.py:431
  26.5 1.1 %collective-permute-done.6.other_ref = f32[32,128]{1,0:T(8,128)S(1)} collective-permute-done((f32[32,128]{1,0:T(8,128)S(1)}, f32[32,128]{1,0:T(8,128)S(1)}, u32[]{:S(2)}, u32[]{:S(2)}) %collective-permute-start.6) | collective-permute-done | bytes 16416 | tf_op jit(solution)/shard_map/ppermute | solution.py:353
  27.6 0.0 copy-done.4
  27.6 17.8 %main.1 = bf16[12,4,32,256]{3,2,1,0:T(8,128)(2,1)} custom-call(s32[16,12]{1,0:T(8,128)S(1)} %copy-done.4, f32[2048,384]{1,0:T(8,128)S(1)} %raw.2.low_ref, f32[2048,384]{1,0:T(8,128)S(1)} %raw.3.high_ref, f32[32,128]{1,0:T(8,128)S(1)} %pad_maximum_fusion.1.st_ref, f32[32,128]{1,0:T(8,128)S(1)} %collective-permute-done.6.other_ref, f32[1,32]{1,0:T(1,128)S(1)} %bitcast.12, ...), custom_call_target="tpu_custom_call" | custom-call | tf_op jit(solution)/shard_map/main/pallas_call | solution.py:459
  (12 shorter events, 0.1 us)
Async XLA Ops:
  0.9 10.0 %collective-permute-start = (bf16[16,12,256]{2,1,0:T(8,128)(2,1)S(1)}, bf16[16,12,256]{2,1,0:T(8,128)(2,1)S(1)}, u32[]{:S(2)}, u32[]{:S(2)}) collective-permute-start(bf16[16,12,256]{2,1,0:T(8,128)(2,1)S(1)} %copy.16.own_ref), channel_id=1, source_target_pairs={{0,1},{1,0},{2,3},{3,2},{4,5},{5,4},{6,7},{7,6},{8,9},{9,8},{10,11... | collective-permute-start | bytes 294920 | tf_op jit(solution)/shard_map/ppermute | solution.py:353
  1.5 9.5 %collective-permute-start.1 = (bf16[16,12,256]{2,1,0:T(8,128)(2,1)S(1)}, bf16[16,12,256]{2,1,0:T(8,128)(2,1)S(1)}, u32[]{:S(2)}, u32[]{:S(2)}) collective-permute-start(bf16[16,12,256]{2,1,0:T(8,128)(2,1)S(1)} %copy.16.own_ref), channel_id=1, source_target_pairs={{0,0},{1,2},{2,1},{3,4},{4,3},{5,6},{6,5},{7,8},{8,7},{9,10},{10,9... | collective-permute-start | bytes 294920 | tf_op jit(solution)/shard_map/ppermute | solution.py:348
  2.2 5.6 %collective-permute-start.2 = (bf16[16,3,256]{2,1,0:T(4,128)(2,1)S(1)}, bf16[16,3,256]{2,1,0:T(4,128)(2,1)S(1)}, u32[]{:S(2)}, u32[]{:S(2)}) collective-permute-start(bf16[16,3,256]{2,1,0:T(4,128)(2,1)S(1)} %get-tuple-element.44), channel_id=1, source_target_pairs={{0,2},{1,0},{2,4},{3,1},{4,6},{5,3},{6,8},{7,5},{8,10},{9,7},{10,1... | collective-permute-start | bytes 73736 | tf_op jit(solution)/shard_map/ppermute | solution.py:348
  6.0 4.9 %collective-permute-start.3 = (bf16[16,3,256]{2,1,0:T(4,128)(2,1)S(1)}, bf16[16,3,256]{2,1,0:T(4,128)(2,1)S(1)}, u32[]{:S(2)}, u32[]{:S(2)}) collective-permute-start(bf16[16,3,256]{2,1,0:T(4,128)(2,1)S(1)} %get-tuple-element.43), channel_id=1, source_target_pairs={{0,1},{1,3},{2,0},{3,5},{4,2},{5,7},{6,4},{7,9},{8,6},{9,11},{10,8... | collective-permute-start | bytes 73736 | tf_op jit(solution)/shard_map/ppermute | solution.py:348
  14.0 11.7 %copy-start = (bf16[3,3,3,32,32]{4,3,2,1,0:T(8,128)(2,1)S(1)}, bf16[3,3,3,32,32]{4,3,2,1,0:T(8,128)(2,1)}, u32[]{:S(2)}) copy-start(bf16[3,3,3,32,32]{4,3,2,1,0:T(8,128)(2,1)} %param.17) | copy-start | bytes 165892
  14.0 5.0 %collective-permute-start.4 = (f32[32,128]{1,0:T(8,128)S(1)}, f32[32,128]{1,0:T(8,128)S(1)}, u32[]{:S(2)}, u32[]{:S(2)}) collective-permute-start(f32[32,128]{1,0:T(8,128)S(1)} %get-tuple-element.24), channel_id=1, source_target_pairs={{0,2},{1,3},{2,0},{3,1},{4,6},{5,7},{6,4},{7,5},{8,10},{9,11},{10,... | collective-permute-start | bytes 49160 | tf_op jit(solution)/shard_map/ppermute | solution.py:353
  17.0 0.9 %copy-start.2 = (bf16[3,3,32,32]{3,2,1,0:T(8,128)(2,1)S(1)}, bf16[3,3,32,32]{3,2,1,0:T(8,128)(2,1)}, u32[]{:S(2)}) copy-start(bf16[3,3,32,32]{3,2,1,0:T(8,128)(2,1)} %param.14) | copy-start | bytes 55300
  17.9 0.9 %copy-start.3 = (bf16[3,3,32,32]{3,2,1,0:T(8,128)(2,1)S(1)}, bf16[3,3,32,32]{3,2,1,0:T(8,128)(2,1)}, u32[]{:S(2)}) copy-start(bf16[3,3,32,32]{3,2,1,0:T(8,128)(2,1)} %param.15) | copy-start | bytes 55300
  19.1 3.8 %collective-permute-start.5 = (f32[32,128]{1,0:T(8,128)S(1)}, f32[32,128]{1,0:T(8,128)S(1)}, u32[]{:S(2)}, u32[]{:S(2)}) collective-permute-start(f32[32,128]{1,0:T(8,128)S(1)} %pad_maximum_fusion), channel_id=1, source_target_pairs={{0,4},{1,5},{2,6},{3,7},{4,0},{5,1},{6,2},{7,3},{8,12},{9,13},{10,... | collective-permute-start | bytes 49160 | tf_op jit(solution)/shard_map/ppermute | solution.py:353
  20.8 0.9 %copy-start.1 = (bf16[3,3,3,32,32]{4,3,2,1,0:T(8,128)(2,1)S(1)}, bf16[3,3,3,32,32]{4,3,2,1,0:T(8,128)(2,1)}, u32[]{:S(2)}) copy-start(bf16[3,3,3,32,32]{4,3,2,1,0:T(8,128)(2,1)} %param.16) | copy-start | bytes 165892
  22.7 4.9 %copy-start.4 = (s32[16,12]{1,0:T(8,128)S(1)}, s32[16,12]{1,0:T(8,128)}, u32[]{:S(2)}) copy-start(s32[16,12]{1,0:T(8,128)} %shifts.1) | copy-start | bytes 2308
  22.7 4.9 %copy-start.5 = (f32[32]{0:T(128)S(1)}, f32[32]{0:T(128)}, u32[]{:S(2)}) copy-start(f32[32]{0:T(128)} %param.12) | copy-start | bytes 388
  22.7 4.9 %copy-start.6 = (f32[32]{0:T(128)S(1)}, f32[32]{0:T(128)}, u32[]{:S(2)}) copy-start(f32[32]{0:T(128)} %param.13) | copy-start | bytes 388
  22.9 4.7 %collective-permute-start.6 = (f32[32,128]{1,0:T(8,128)S(1)}, f32[32,128]{1,0:T(8,128)S(1)}, u32[]{:S(2)}, u32[]{:S(2)}) collective-permute-start(f32[32,128]{1,0:T(8,128)S(1)} %pad_maximum_fusion.1.st_ref), channel_id=1, source_target_pairs={{0,8},{1,9},{2,10},{3,11},{4,12},{5,13},{6,14},{7,15},{8,0},{9,1},... | collective-permute-start | bytes 49160 | tf_op jit(solution)/shard_map/ppermute | solution.py:353

commit v5 on v4

--- a/solution.py
+++ b/solution.py
@@ -253,7 +253,8 @@
         if i < 4:
             one_plane(2 * i + 4, 0)
             one_plane(2 * i + 5, 0)
-    final(0, 0)
+        if i == 3:
+            final(0, 0)
     final(1, 0)
 
 

time: 45.8 us -> 48.2 us (1.052)
  Pallas kernels: 23.3 us -> 25.6 us
    pallas_call x1, Pallas kernels: 17.8 us -> 20.1 us  [shards(): pl.pallas_call(main_kernel, name='main', out_shape=jax.ShapeDtypeStruct((...]
where the time goes in v5:
time: 48.2 us; the launch traced here: 47.9 us
  Pallas kernels  25.6 us (53%)
  starting transfers between devices  12.6 us (26%)
  waiting for transfers between devices  4.92 us (10%)
  local copies, waits for them, and re-layouts  4.38 us (9%)
    pallas_call x1, Pallas kernels, shards(): pl.pallas_call(main_kernel, name='main', out_shape=jax.ShapeDtypeStruct((...  20.1 us
    ppermute x4, starting transfers between devices, swap(): return lax.ppermute(value, axis, [(i, i ^ bit) for i in range(count)])  7.93 us
    ppermute x3, starting transfers between devices, send(): return lax.ppermute(value, axis, pairs)  4.68 us
    ppermute x3, waiting for transfers between devices, send(): return lax.ppermute(value, axis, pairs)  3.65 us
    unnamed x15, local copies, waits for them, and re-layouts  3.63 us
    pallas_call x1, Pallas kernels, shards(): pl.pallas_call(stats_kernel, name='stats', out_shape=(jax.ShapeDtypeStruc...  3.06 us
    pallas_call x4, Pallas kernels, weights(): pl.pallas_call(kernel, name=kernel.__name__, out_shape=shapes, in_specs=[...  1.35 us
    ppermute x4, waiting for transfers between devices, swap(): return lax.ppermute(value, axis, [(i, i ^ bit) for i in range(count)])  1.26 us
  transfers between devices with their start and end apart: 7, of which 4 were waited for; matrix products, arithmetic and copies ran while one was open for 2% of the time, Pallas kernels for 5%

profile of v5, /device:TPU:0, one launch (start us, length us, event | category | flops | bytes accessed | tf_op | source)
XLA Modules:
  0.0 47.9 jit_solution(9816273025957900018)
XLA Ops:
  0.0 0.9 %copy.11 = bf16[16,4,3,256]{3,0,2,1:T(8,128)(2,1)S(1)} copy(bf16[16,4,3,256]{3,1,2,0:T(4,128)(2,1)} %param.9) | data formatting | bytes 196608 | tf_op args[0]
  0.9 0.5 %collective-permute-start = (bf16[16,12,256]{2,1,0:T(8,128)(2,1)S(1)}, bf16[16,12,256]{2,1,0:T(8,128)(2,1)S(1)}, u32[]{:S(2)}, u32[]{:S(2)}) collective-permute-start(bf16[16,12,256]{2,1,0:T(8,128)(2,1)S(1)} %copy.16.own_ref), channel_id=1, source_target_pairs={{0,1},{1,0},{2,3},{3,2},{4,5},{5,4},{6,7},{7,6},{8,9},{9,8},{10,11... | collective-permute-start | bytes 294920 | tf_op jit(solution)/shard_map/ppermute | solution.py:354
  1.5 0.7 %collective-permute-start.1 = (bf16[16,12,256]{2,1,0:T(8,128)(2,1)S(1)}, bf16[16,12,256]{2,1,0:T(8,128)(2,1)S(1)}, u32[]{:S(2)}, u32[]{:S(2)}) collective-permute-start(bf16[16,12,256]{2,1,0:T(8,128)(2,1)S(1)} %copy.16.own_ref), channel_id=1, source_target_pairs={{0,0},{1,2},{2,1},{3,4},{4,3},{5,6},{6,5},{7,8},{8,7},{9,10},{10,9... | collective-permute-start | bytes 294920 | tf_op jit(solution)/shard_map/ppermute | solution.py:349
  2.2 3.8 %collective-permute-start.2 = (bf16[16,3,256]{2,1,0:T(4,128)(2,1)S(1)}, bf16[16,3,256]{2,1,0:T(4,128)(2,1)S(1)}, u32[]{:S(2)}, u32[]{:S(2)}) collective-permute-start(bf16[16,3,256]{2,1,0:T(4,128)(2,1)S(1)} %get-tuple-element.44), channel_id=1, source_target_pairs={{0,2},{1,0},{2,4},{3,1},{4,6},{5,3},{6,8},{7,5},{8,10},{9,7},{10,1... | collective-permute-start | bytes 73736 | tf_op jit(solution)/shard_map/ppermute | solution.py:349
  6.0 0.2 collective-permute-start.3
  6.2 0.7 %reshape.19.w_ref = bf16[27,32]{1,0:T(8,128)(2,1)S(1)} reshape(bf16[3,3,3,32]{3,2,1,0:T(4,128)(2,1)} %bitcast.15) | data formatting | bytes 3456 | tf_op jit(solution)/shard_map/reshape | solution.py:400
  6.9 0.3 color_weights_kernel.1.w_ref.w1_ref
  7.3 0.5 %collective-permute-done.2.near_ref = bf16[16,3,256]{2,1,0:T(4,128)(2,1)S(1)} collective-permute-done((bf16[16,3,256]{2,1,0:T(4,128)(2,1)S(1)}, bf16[16,3,256]{2,1,0:T(4,128)(2,1)S(1)}, u32[]{:S(2)}, u32[]{:S(2)}) %collective-permute-start.2) | collective-permute-done | bytes 24608 | tf_op jit(solution)/shard_map/ppermute | solution.py:349
  7.8 3.1 %collective-permute-done.3.next_ref = bf16[16,3,256]{2,1,0:T(4,128)(2,1)S(1)} collective-permute-done((bf16[16,3,256]{2,1,0:T(4,128)(2,1)S(1)}, bf16[16,3,256]{2,1,0:T(4,128)(2,1)S(1)}, u32[]{:S(2)}, u32[]{:S(2)}) %collective-permute-start.3) | collective-permute-done | bytes 24608 | tf_op jit(solution)/shard_map/ppermute | solution.py:349
  10.9 0.0 collective-permute-done.pair_ref
  10.9 0.0 collective-permute-done.1.far_ref
  10.9 3.1 %stats.1 = (bf16[4096,128]{1,0:T(8,128)(2,1)S(1)}, f32[32,128]{1,0:T(8,128)S(1)}) custom-call(bf16[16,12,256]{2,1,0:T(8,128)(2,1)S(1)} %copy.16.own_ref, bf16[16,12,256]{2,1,0:T(8,128)(2,1)S(1)} %collective-permute-done.pair_ref, bf16[16,12,256]{2,1,0:T(8,128)(2,1)S(1)} %collective-permute-done.1.far_ref, ...), custom_call_target="tpu_custom_call" | custom-call | tf_op jit(solution)/shard_map/stats/pallas_call | solution.py:403
  14.0 3.0 %collective-permute-start.4 = (f32[32,128]{1,0:T(8,128)S(1)}, f32[32,128]{1,0:T(8,128)S(1)}, u32[]{:S(2)}, u32[]{:S(2)}) collective-permute-start(f32[32,128]{1,0:T(8,128)S(1)} %get-tuple-element.24), channel_id=1, source_target_pairs={{0,2},{1,3},{2,0},{3,1},{4,6},{5,7},{6,4},{7,5},{8,10},{9,11},{10,... | collective-permute-start | bytes 49160 | tf_op jit(solution)/shard_map/ppermute | solution.py:354
  17.0 0.9 %copy-done.2 = bf16[3,3,32,32]{3,2,1,0:T(8,128)(2,1)S(1)} copy-done((bf16[3,3,32,32]{3,2,1,0:T(8,128)(2,1)S(1)}, bf16[3,3,32,32]{3,2,1,0:T(8,128)(2,1)}, u32[]{:S(2)}) %copy-start.2) | copy-done | bytes 18456
  17.9 0.9 %copy-done.3 = bf16[3,3,32,32]{3,2,1,0:T(8,128)(2,1)S(1)} copy-done((bf16[3,3,32,32]{3,2,1,0:T(8,128)(2,1)S(1)}, bf16[3,3,32,32]{3,2,1,0:T(8,128)(2,1)}, u32[]{:S(2)}) %copy-start.3) | copy-done | bytes 18456
  18.7 0.3 feature_weights_kernel.1
  19.0 0.0 collective-permute-done.4
  19.1 1.7 %collective-permute-start.5 = (f32[32,128]{1,0:T(8,128)S(1)}, f32[32,128]{1,0:T(8,128)S(1)}, u32[]{:S(2)}, u32[]{:S(2)}) collective-permute-start(f32[32,128]{1,0:T(8,128)S(1)} %pad_maximum_fusion), channel_id=1, source_target_pairs={{0,4},{1,5},{2,6},{3,7},{4,0},{5,1},{6,2},{7,3},{8,12},{9,13},{10,... | collective-permute-start | bytes 49160 | tf_op jit(solution)/shard_map/ppermute | solution.py:354
  20.8 0.9 %copy-done.1 = bf16[3,3,3,32,32]{4,3,2,1,0:T(8,128)(2,1)S(1)} copy-done((bf16[3,3,3,32,32]{4,3,2,1,0:T(8,128)(2,1)S(1)}, bf16[3,3,3,32,32]{4,3,2,1,0:T(8,128)(2,1)}, u32[]{:S(2)}) %copy-start.1) | copy-done | bytes 55320
  21.7 0.4 hidden_weights_kernel.1.ca_hbm
  22.1 0.6 %raw.2.low_ref = f32[2048,384]{1,0:T(8,128)S(1)} custom-call(bf16[4096,128]{1,0:T(8,128)(2,1)S(1)} %get-tuple-element.36.pt_ref, bf16[128,384]{1,0:T(8,128)(2,1)S(1)} %color_weights_kernel.1.w_ref.w1_ref), custom_call_target="tpu_custom_call" | custom-call | flops 201326592 | bytes 4000000 | tf_op jit(solution)/shard_map/raw/pallas_call | solution.py:432
  22.7 0.0 copy-start.4
  22.7 0.0 copy-start.5
  22.7 0.0 copy-start.6
  22.7 0.2 collective-permute-done.5
  22.9 2.8 %collective-permute-start.6 = (f32[32,128]{1,0:T(8,128)S(1)}, f32[32,128]{1,0:T(8,128)S(1)}, u32[]{:S(2)}, u32[]{:S(2)}) collective-permute-start(f32[32,128]{1,0:T(8,128)S(1)} %pad_maximum_fusion.1.st_ref), channel_id=1, source_target_pairs={{0,8},{1,9},{2,10},{3,11},{4,12},{5,13},{6,14},{7,15},{8,0},{9,1},... | collective-permute-start | bytes 49160 | tf_op jit(solution)/shard_map/ppermute | solution.py:354
  25.7 0.3 final_weights_kernel.1.cb_hbm
  26.0 0.5 %raw.3.high_ref = f32[2048,384]{1,0:T(8,128)S(1)} custom-call(bf16[4096,128]{1,0:T(8,128)(2,1)S(1)} %get-tuple-element.36.pt_ref, bf16[128,384]{1,0:T(8,128)(2,1)S(1)} %color_weights_kernel.1.w_ref.w1_ref), custom_call_target="tpu_custom_call" | custom-call | flops 201326592 | bytes 4000000 | tf_op jit(solution)/shard_map/raw/pallas_call | solution.py:432
  26.5 1.1 %collective-permute-done.6.other_ref = f32[32,128]{1,0:T(8,128)S(1)} collective-permute-done((f32[32,128]{1,0:T(8,128)S(1)}, f32[32,128]{1,0:T(8,128)S(1)}, u32[]{:S(2)}, u32[]{:S(2)}) %collective-permute-start.6) | collective-permute-done | bytes 16416 | tf_op jit(solution)/shard_map/ppermute | solution.py:354
  27.6 0.0 copy-done.4
  27.6 0.0 copy-done.6
  27.6 20.1 %main.1 = bf16[12,4,32,256]{3,2,1,0:T(8,128)(2,1)} custom-call(s32[16,12]{1,0:T(8,128)S(1)} %copy-done.4, f32[2048,384]{1,0:T(8,128)S(1)} %raw.2.low_ref, f32[2048,384]{1,0:T(8,128)S(1)} %raw.3.high_ref, f32[32,128]{1,0:T(8,128)S(1)} %pad_maximum_fusion.1.st_ref, f32[32,128]{1,0:T(8,128)S(1)} %collective-permute-done.6.other_ref, f32[1,32]{1,0:T(1,128)S(1)} %bitcast.12, ...), custom_call_target="tpu_custom_call" | custom-call | tf_op jit(solution)/shard_map/main/pallas_call | solution.py:460
  (12 shorter events, 0.1 us)
Async XLA Ops:
  0.9 10.0 %collective-permute-start = (bf16[16,12,256]{2,1,0:T(8,128)(2,1)S(1)}, bf16[16,12,256]{2,1,0:T(8,128)(2,1)S(1)}, u32[]{:S(2)}, u32[]{:S(2)}) collective-permute-start(bf16[16,12,256]{2,1,0:T(8,128)(2,1)S(1)} %copy.16.own_ref), channel_id=1, source_target_pairs={{0,1},{1,0},{2,3},{3,2},{4,5},{5,4},{6,7},{7,6},{8,9},{9,8},{10,11... | collective-permute-start | bytes 294920 | tf_op jit(solution)/shard_map/ppermute | solution.py:354
  1.5 9.5 %collective-permute-start.1 = (bf16[16,12,256]{2,1,0:T(8,128)(2,1)S(1)}, bf16[16,12,256]{2,1,0:T(8,128)(2,1)S(1)}, u32[]{:S(2)}, u32[]{:S(2)}) collective-permute-start(bf16[16,12,256]{2,1,0:T(8,128)(2,1)S(1)} %copy.16.own_ref), channel_id=1, source_target_pairs={{0,0},{1,2},{2,1},{3,4},{4,3},{5,6},{6,5},{7,8},{8,7},{9,10},{10,9... | collective-permute-start | bytes 294920 | tf_op jit(solution)/shard_map/ppermute | solution.py:349
  2.2 5.6 %collective-permute-start.2 = (bf16[16,3,256]{2,1,0:T(4,128)(2,1)S(1)}, bf16[16,3,256]{2,1,0:T(4,128)(2,1)S(1)}, u32[]{:S(2)}, u32[]{:S(2)}) collective-permute-start(bf16[16,3,256]{2,1,0:T(4,128)(2,1)S(1)} %get-tuple-element.44), channel_id=1, source_target_pairs={{0,2},{1,0},{2,4},{3,1},{4,6},{5,3},{6,8},{7,5},{8,10},{9,7},{10,1... | collective-permute-start | bytes 73736 | tf_op jit(solution)/shard_map/ppermute | solution.py:349
  6.0 4.9 %collective-permute-start.3 = (bf16[16,3,256]{2,1,0:T(4,128)(2,1)S(1)}, bf16[16,3,256]{2,1,0:T(4,128)(2,1)S(1)}, u32[]{:S(2)}, u32[]{:S(2)}) collective-permute-start(bf16[16,3,256]{2,1,0:T(4,128)(2,1)S(1)} %get-tuple-element.43), channel_id=1, source_target_pairs={{0,1},{1,3},{2,0},{3,5},{4,2},{5,7},{6,4},{7,9},{8,6},{9,11},{10,8... | collective-permute-start | bytes 73736 | tf_op jit(solution)/shard_map/ppermute | solution.py:349
  14.0 11.7 %copy-start = (bf16[3,3,3,32,32]{4,3,2,1,0:T(8,128)(2,1)S(1)}, bf16[3,3,3,32,32]{4,3,2,1,0:T(8,128)(2,1)}, u32[]{:S(2)}) copy-start(bf16[3,3,3,32,32]{4,3,2,1,0:T(8,128)(2,1)} %param.17) | copy-start | bytes 165892
  14.0 5.0 %collective-permute-start.4 = (f32[32,128]{1,0:T(8,128)S(1)}, f32[32,128]{1,0:T(8,128)S(1)}, u32[]{:S(2)}, u32[]{:S(2)}) collective-permute-start(f32[32,128]{1,0:T(8,128)S(1)} %get-tuple-element.24), channel_id=1, source_target_pairs={{0,2},{1,3},{2,0},{3,1},{4,6},{5,7},{6,4},{7,5},{8,10},{9,11},{10,... | collective-permute-start | bytes 49160 | tf_op jit(solution)/shard_map/ppermute | solution.py:354
  17.0 0.9 %copy-start.2 = (bf16[3,3,32,32]{3,2,1,0:T(8,128)(2,1)S(1)}, bf16[3,3,32,32]{3,2,1,0:T(8,128)(2,1)}, u32[]{:S(2)}) copy-start(bf16[3,3,32,32]{3,2,1,0:T(8,128)(2,1)} %param.14) | copy-start | bytes 55300
  17.9 0.9 %copy-start.3 = (bf16[3,3,32,32]{3,2,1,0:T(8,128)(2,1)S(1)}, bf16[3,3,32,32]{3,2,1,0:T(8,128)(2,1)}, u32[]{:S(2)}) copy-start(bf16[3,3,32,32]{3,2,1,0:T(8,128)(2,1)} %param.15) | copy-start | bytes 55300
  19.1 3.8 %collective-permute-start.5 = (f32[32,128]{1,0:T(8,128)S(1)}, f32[32,128]{1,0:T(8,128)S(1)}, u32[]{:S(2)}, u32[]{:S(2)}) collective-permute-start(f32[32,128]{1,0:T(8,128)S(1)} %pad_maximum_fusion), channel_id=1, source_target_pairs={{0,4},{1,5},{2,6},{3,7},{4,0},{5,1},{6,2},{7,3},{8,12},{9,13},{10,... | collective-permute-start | bytes 49160 | tf_op jit(solution)/shard_map/ppermute | solution.py:354
  20.8 0.9 %copy-start.1 = (bf16[3,3,3,32,32]{4,3,2,1,0:T(8,128)(2,1)S(1)}, bf16[3,3,3,32,32]{4,3,2,1,0:T(8,128)(2,1)}, u32[]{:S(2)}) copy-start(bf16[3,3,3,32,32]{4,3,2,1,0:T(8,128)(2,1)} %param.16) | copy-start | bytes 165892
  22.7 4.9 %copy-start.4 = (s32[16,12]{1,0:T(8,128)S(1)}, s32[16,12]{1,0:T(8,128)}, u32[]{:S(2)}) copy-start(s32[16,12]{1,0:T(8,128)} %shifts.1) | copy-start | bytes 2308
  22.7 4.9 %copy-start.5 = (f32[32]{0:T(128)S(1)}, f32[32]{0:T(128)}, u32[]{:S(2)}) copy-start(f32[32]{0:T(128)} %param.12) | copy-start | bytes 388
  22.7 4.9 %copy-start.6 = (f32[32]{0:T(128)S(1)}, f32[32]{0:T(128)}, u32[]{:S(2)}) copy-start(f32[32]{0:T(128)} %param.13) | copy-start | bytes 388
  22.9 4.7 %collective-permute-start.6 = (f32[32,128]{1,0:T(8,128)S(1)}, f32[32,128]{1,0:T(8,128)S(1)}, u32[]{:S(2)}, u32[]{:S(2)}) collective-permute-start(f32[32,128]{1,0:T(8,128)S(1)} %pad_maximum_fusion.1.st_ref), channel_id=1, source_target_pairs={{0,8},{1,9},{2,10},{3,11},{4,12},{5,13},{6,14},{7,15},{8,0},{9,1},... | collective-permute-start | bytes 49160 | tf_op jit(solution)/shard_map/ppermute | solution.py:354
